TPU v7x, 256 devices: a whole 4x4x8 slice. The times are simulated.
256 devices in a mesh: blk: 32 (over x, y, core), sub: 8 (over z).
Axes of the slice: x: 4, y: 4, z: 8, core: 2. Of those that a mesh axis runs over, the one named last changes fastest.
Arguments:
- adjoint: float32 [6, 32, 32, 64, 128], P(None, 'blk', 'sub'), may hold values from -6 to 6
- source: float32 [6, 32, 32, 64, 128], P(None, 'blk', 'sub'), may hold values from -6 to 6
- cell_coef: float32 [4, 32, 32, 64, 128], P(None, 'blk', 'sub'), may hold values from 0.5 to 2
- flux_jacobian: float32 [32, 3, 2, 6, 6], P('blk'), may hold values from -2.5 to 2.5
- fringe_dest: int32 [1048576, 1], P(('blk', 'sub')), may hold values from 0 to 31; in each aligned block of 4096 rows (0 to 4095, 4096 to 8191, ...) at most 256 rows name the same one
- fringe_cell: int32 [1048576], P(('blk', 'sub')), may hold values from 0 to 32767
- fringe_base: int32 [1048576], P(('blk', 'sub')), may hold values from 0 to 24446, as said below
- fringe_frac: float32 [3, 1048576], P(None, ('blk', 'sub')), may hold values from 0 to 1
Outputs:
- adjoint_residual: float32 [6, 32, 32, 64, 128], P(None, 'blk', 'sub')
Inputs may be any that keep to these rules, and one draw needn't show every extreme that they name: `fringe_dest`: in each aligned block of 4096 rows (the records of one device), no blk index is named by more than 256 rows. `fringe_base`: A donor base cell (n, i, j, k) in the local numbering always has i < 3, j < 63 and k < 127, so all eight corners lie on the record's own device and block.
All inputs are finite; a program needn't handle non-finite values.
Results may differ from a plain program's by a relative error of at most 0.0001.
Values sent between devices are 32-bit elements; how exact they have to be, the bound alone decides.
A program may use at most 128 MiB of HBM per device.

v0:
```python
import jax
import jax.numpy as jnp
from jax import lax
from jax.sharding import PartitionSpec as P

CAP = 256


def padded_2(block, sides, width):
    for axis, dim in sides:
        count = lax.axis_size(axis)
        forward = [(i, i + 1) for i in range(count - 1)]
        backward = [(target, source) for source, target in forward]
        low = lax.ppermute(
            lax.slice_in_dim(block, block.shape[dim] - width, None, axis=dim), axis, forward
        )
        high = lax.ppermute(lax.slice_in_dim(block, 0, width, axis=dim), axis, backward)
        block = jnp.concatenate([low, block, high], axis=dim)
    return block


def corner_weights(fractions, row_stride, col_stride):
    listing = []
    for step_i in range(2):
        weight_i = fractions[0] if step_i else 1.0 - fractions[0]
        for step_j in range(2):
            weight_j = fractions[1] if step_j else 1.0 - fractions[1]
            for step_k in range(2):
                weight_k = fractions[2] if step_k else 1.0 - fractions[2]
                offset = step_i * row_stride + step_j * col_stride + step_k
                listing.append((offset, weight_i * weight_j * weight_k))
    return listing


def shift_next(grid_field, grid_axis):
    length = grid_field.shape[grid_axis]
    sliced = lax.slice_in_dim(grid_field, 1, length, axis=grid_axis)
    widths = [(0, 0)] * grid_field.ndim
    widths[grid_axis] = (0, 1)
    return jnp.pad(sliced, widths)


def shift_prev(grid_field, grid_axis):
    length = grid_field.shape[grid_axis]
    sliced = lax.slice_in_dim(grid_field, 0, length - 1, axis=grid_axis)
    widths = [(0, 0)] * grid_field.ndim
    widths[grid_axis] = (1, 0)
    return jnp.pad(sliced, widths)


def transpose_apply(matrix, grid_field):
    total = None
    for var in range(grid_field.shape[0]):
        factor = jnp.transpose(matrix[:, var, :])[:, :, None, None, None]
        term = factor * grid_field[var][None]
        total = term if total is None else total + term
    return total


def slab_rim(grid_field):
    return padded_2(grid_field, (("sub", 2),), 1)


def transposed_sweep(centre, padded, cell_coef, flux_jacobian):
    running = cell_coef[0] * centre
    for direction in range(3):
        source_grid = padded if direction == 0 else centre
        upper_term = transpose_apply(flux_jacobian[:, direction, 0], source_grid)
        lower_term = transpose_apply(flux_jacobian[:, direction, 1], source_grid)
        if direction == 0:
            from_next = upper_term[:, :, 2:]
            from_prev = lower_term[:, :, :-2]
        else:
            from_next = shift_next(upper_term, 2 + direction)
            from_prev = shift_prev(lower_term, 2 + direction)
        running = running + cell_coef[direction + 1] * (from_next + from_prev)
    return running


def per_device(
    adjoint, source, cell_coef, flux_jacobian, fringe_dest, fringe_cell, fringe_base, fringe_frac
):
    var_count = adjoint.shape[0]
    row_stride = adjoint.shape[3] * adjoint.shape[4]
    col_stride = adjoint.shape[4]
    cell_count = adjoint.shape[1] * adjoint.shape[2] * row_stride
    groups = lax.axis_size("blk")
    slot_total = groups * CAP
    flat_field = adjoint.reshape(var_count, cell_count)
    dest_index = fringe_dest[:, 0]
    onehot = (jnp.arange(groups, dtype=jnp.int32)[:, None] == dest_index[None, :]).astype(jnp.int32)
    before = jnp.cumsum(onehot, axis=1) - onehot
    rank_in = jnp.sum(before * onehot, axis=0)
    slot_index = dest_index * CAP + rank_in
    weights = corner_weights(fringe_frac, row_stride, col_stride)
    land_slots = (
        jnp.zeros((1, slot_total), jnp.float32)
        .at[:, slot_index]
        .set(fringe_cell.astype(jnp.float32)[None, :])
    )
    land_slots = land_slots.reshape(1, groups, CAP)
    interp_value = jnp.zeros((var_count, fringe_cell.shape[0]), jnp.float32)
    for offset, weight in weights:
        interp_value = interp_value + weight * flat_field[:, fringe_base + offset]
    packed = jnp.zeros((var_count, slot_total), jnp.float32).at[:, slot_index].set(interp_value)
    packed = packed.reshape(var_count, groups, CAP)
    got_values, got_land = (
        lax.all_to_all(packed, "blk", split_axis=1, concat_axis=1, tiled=True),
        lax.all_to_all(land_slots, "blk", split_axis=1, concat_axis=1, tiled=True),
    )
    incoming = got_values.reshape(var_count, slot_total)
    landing = got_land.reshape(slot_total).astype(jnp.int32)
    merged = flat_field.at[:, landing].add(incoming).reshape(adjoint.shape)
    image = transposed_sweep(merged, slab_rim(merged), cell_coef, flux_jacobian)
    residual = source - image
    res_flat = residual.reshape(var_count, cell_count)
    at_receivers = res_flat[:, landing].reshape(var_count, groups, CAP)
    returned = lax.all_to_all(at_receivers, "blk", split_axis=1, concat_axis=1, tiled=True)
    returned = returned.reshape(var_count, slot_total)[:, slot_index]
    result = res_flat
    for offset, weight in weights:
        result = result.at[:, fringe_base + offset].add(weight * returned)
    return result.reshape(adjoint.shape)


def solution(mesh):
    return jax.shard_map(
        per_device,
        mesh=mesh,
        in_specs=(
            P(None, "blk", "sub", None, None),
            P(None, "blk", "sub", None, None),
            P(None, "blk", "sub", None, None),
            P("blk", None, None, None, None),
            P(("blk", "sub"), None),
            P(("blk", "sub")),
            P(("blk", "sub")),
            P(None, ("blk", "sub")),
        ),
        out_specs=P(None, "blk", "sub", None, None),
        check_vma=False,
    )
```

profile of v0, /device:TPU:1, one launch (start us, length us, event | category | flops | bytes accessed | tf_op | source)
XLA Modules:
  0.0 732.3 jit_solution(6983065893047877612)
XLA Ops:
  0.9 9.2 %reduce-window.6 = s32[32,32,128]{2,1,0:T(8,128)S(1)} reduce-window(s32[32,32,128]{2,1,0:T(8,128)S(1)} %fusion.2, s32[]{:T(128)} %constant.13.clone.1), window={size=1x1x128 pad=0_0x0_0x127_0}, to_apply=%region_0.0 | reduce-window | flops 16646144 | bytes 1048580 | tf_op jit(solution)/shard_map/reduce-window
  11.4 16.1 %scatter_custom_fusion = f32[8192]{0:T(1024)} fusion(s32[4096]{0:T(1024)S(1)} %bitcast.196, f32[4096]{0:T(1024)S(1)} %convert_element_type.30, f32[]{:T(128)} %constant.11.clone.1), kind=kCustom, calls=%fused_computation.70 | custom fusion | bytes 32772 | tf_op jit(solution)/shard_map/scatter | solution.py:99
  27.5 8.6 %all-to-all-start = ((f32[1,32,256]{2,0,1:T(1,128)}), f32[1,32,256]{2,0,1:T(1,128)}, u32[]{:S(2)}, u32[]{:S(2)}) async-start(f32[1,32,256]{2,0,1:T(1,128)} %bitcast.5), calls=%async_computation | async-start | bytes 65536 | tf_op jit(solution)/shard_map/all_to_all | solution.py:109
  38.2 8.8 %copy.41 = f32[6,1,4,64,128]{0,4,3,2,1:T(8,128)} copy(f32[6,1,4,64,128]{4,3,2,1,0:T(8,128)S(1)} %copy-done) | data formatting | bytes 1572864 | tf_op args[0]
  46.9 16.5 %gather_fusion = f32[4096,6]{1,0:T(8,128)S(1)} fusion(f32[6,32768]{0,1:T(8,128)} %bitcast.145, s32[4096]{0:T(1024)S(1)} %get-tuple-element.89), kind=kCustom, calls=%fused_computation | custom fusion | bytes 212992 | tf_op jit(solution)/shard_map/gather | solution.py:104
  64.1 16.5 %gather_fusion.1 = f32[4096,6]{1,0:T(8,128)S(1)} fusion(f32[6,32768]{0,1:T(8,128)} %bitcast.146, s32[4096]{0:T(1024)S(1)} %get-tuple-element.88), kind=kCustom, calls=%fused_computation.1 | custom fusion | bytes 212992 | tf_op jit(solution)/shard_map/gather | solution.py:104
  81.3 16.5 %gather_fusion.2 = f32[4096,6]{1,0:T(8,128)S(1)} fusion(f32[6,32768]{0,1:T(8,128)} %bitcast.147, s32[4096]{0:T(1024)S(1)} %get-tuple-element.87), kind=kCustom, calls=%fused_computation.2 | custom fusion | bytes 212992 | tf_op jit(solution)/shard_map/gather | solution.py:104
  98.4 16.5 %gather_fusion.3 = f32[4096,6]{1,0:T(8,128)S(1)} fusion(f32[6,32768]{0,1:T(8,128)} %bitcast.148, s32[4096]{0:T(1024)S(1)} %get-tuple-element.86), kind=kCustom, calls=%fused_computation.3 | custom fusion | bytes 212992 | tf_op jit(solution)/shard_map/gather | solution.py:104
  115.6 16.5 %gather_fusion.4 = f32[4096,6]{1,0:T(8,128)S(1)} fusion(f32[6,32768]{0,1:T(8,128)} %bitcast.149, s32[4096]{0:T(1024)S(1)} %get-tuple-element.85), kind=kCustom, calls=%fused_computation.4 | custom fusion | bytes 212992 | tf_op jit(solution)/shard_map/gather | solution.py:104
  132.8 16.5 %gather_fusion.5 = f32[4096,6]{1,0:T(8,128)S(1)} fusion(f32[6,32768]{0,1:T(8,128)} %bitcast.150, s32[4096]{0:T(1024)S(1)} %get-tuple-element.84), kind=kCustom, calls=%fused_computation.5 | custom fusion | bytes 212992 | tf_op jit(solution)/shard_map/gather | solution.py:104
  150.0 16.5 %gather_fusion.6 = f32[4096,6]{1,0:T(8,128)S(1)} fusion(f32[6,32768]{0,1:T(8,128)} %bitcast.151, s32[4096]{0:T(1024)S(1)} %get-tuple-element.83), kind=kCustom, calls=%fused_computation.6 | custom fusion | bytes 212992 | tf_op jit(solution)/shard_map/gather | solution.py:104
  167.2 16.6 %gather_fusion.7 = f32[4096,6]{1,0:T(8,128)S(1)} fusion(f32[6,32768]{0,1:T(8,128)} %bitcast.152, s32[4096]{0:T(1024)S(1)} %get-tuple-element.82), kind=kCustom, calls=%fused_computation.7 | custom fusion | bytes 212992 | tf_op jit(solution)/shard_map/gather | solution.py:104
  187.4 1.7 fusion.3
  189.8 1.5 copy.50
  191.3 12.9 %scatter_custom_fusion.1 = f32[6,8192]{0,1:T(8,128)} fusion(s32[4096]{0:T(1024)} %bitcast.197, f32[4096,6]{1,0:T(8,128)S(1)} %copy.50, f32[]{:T(128)} %constant.11.clone.1), kind=kCustom, calls=%fused_computation.27 | custom fusion | bytes 197120 | tf_op jit(solution)/shard_map/scatter | solution.py:105
  204.2 3.5 copy.51
  207.7 8.0 %all-to-all-start.1 = ((f32[6,32,256]{2,0,1:T(8,128)}), f32[6,32,256]{2,0,1:T(8,128)S(1)}, u32[]{:S(2)}, u32[]{:S(2)}) async-start(f32[6,32,256]{2,0,1:T(8,128)} %copy.51), calls=%async_computation.1 | async-start | bytes 524288 | tf_op jit(solution)/shard_map/all_to_all | solution.py:108
  217.2 7.4 %all-to-all-done.1 = f32[6,32,256]{2,0,1:T(8,128)S(1)} async-done(((f32[6,32,256]{2,0,1:T(8,128)}), f32[6,32,256]{2,0,1:T(8,128)S(1)}, u32[]{:S(2)}, u32[]{:S(2)}) %all-to-all-start.1) | async-done | bytes 196640 | tf_op jit(solution)/shard_map/all_to_all | solution.py:108
  224.6 2.6 copy.52
  227.2 64.3 %scatter_fusion = f32[6,32768]{0,1:T(8,128)} fusion(f32[6,32768]{0,1:T(8,128)} %bitcast.153, s32[8192]{0:T(1024)S(1)} %bitcast.175, f32[8192,6]{1,0:T(8,128)} %copy.52), kind=kCustom, calls=%fused_computation.12 | custom fusion | flops 49152 | bytes 622592 | tf_op jit(solution)/shard_map/scatter-add | solution.py:113
  291.5 57.7 %slice_reduce_fusion.5 = (f32[32768]{0:T(1024)S(1)}, f32[32768]{0:T(1024)S(1)}, f32[32768]{0:T(1024)S(1)}, f32[32768]{0:T(1024)S(1)}, f32[32768]{0:T(1024)S(1)}, /*index=5*/f32[32768]{0:T(1024)S(1)}) fusion(f32[6,32768]{0,1:T(8,128)} %scatter_fusion), kind=kLoop, calls=%fused_computation.26 | loop fusion | bytes 1572864 | tf_op jit(solution)/shard_map/slice | solution.py:55
  351.8 10.1 %copy.53 = f32[6,1,4,64,128]{4,3,2,1,0:T(8,128)S(1)} copy(f32[6,1,4,64,128]{0,4,3,2,1:T(8,128)} %bitcast.154) | data formatting | bytes 1572864 | tf_op jit(solution)/shard_map/reshape | solution.py:113
  362.1 3.5 collective-permute-start
  367.1 1.5 multiply_add_fusion.3
  370.0 2.0 collective-permute-done.1
  374.7 8.8 %copy.57 = f32[6,1,4,64,128]{0,4,3,2,1:T(8,128)} copy(f32[6,1,4,64,128]{4,3,2,1,0:T(8,128)S(1)} %add_subtract_fusion) | data formatting | bytes 1572864 | tf_op jit(solution)/shard_map/sub | solution.py:115
  383.4 33.5 %gather_fusion.8 = f32[8192,6]{1,0:T(8,128)} fusion(f32[6,32768]{0,1:T(8,128)} %bitcast.155, s32[8192]{0:T(1024)S(1)} %copy-done.13), kind=kCustom, calls=%fused_computation.8 | custom fusion | bytes 425984 | tf_op jit(solution)/shard_map/gather | solution.py:117
  416.9 3.5 copy.58
  420.5 5.4 all-to-all-start.2
  425.9 9.0 %all-to-all-done.2 = f32[6,32,256]{2,0,1:T(8,128)S(1)} async-done(((f32[6,32,256]{2,0,1:T(8,128)}), f32[6,32,256]{2,0,1:T(8,128)S(1)}, u32[]{:S(2)}, u32[]{:S(2)}) %all-to-all-start.2) | async-done | bytes 196640 | tf_op jit(solution)/shard_map/all_to_all | solution.py:118
  434.8 2.6 copy.59
  437.5 13.0 %gather_fusion.9 = f32[4096,6]{1,0:T(8,128)S(1)} fusion(f32[6,8192]{0,1:T(8,128)} %bitcast.159, s32[4096]{0:T(1024)S(1)} %broadcast_clamp_fusion.1), kind=kCustom, calls=%fused_computation.9 | custom fusion | bytes 212992 | tf_op jit(solution)/shard_map/gather | solution.py:119
  451.3 2.0 copy.61
  453.3 2.0 copy.63
  455.2 2.0 copy.65
  457.3 2.0 copy.67
  459.3 2.0 copy.69
  461.3 1.9 copy.71
  463.2 2.0 copy.73
  465.9 32.1 %scatter_fusion.1 = f32[6,32768]{0,1:T(8,128)} fusion(f32[6,32768]{0,1:T(8,128)} %bitcast.156, s32[4096]{0:T(1024)S(1)} %copy-done.21, f32[4096,6]{1,0:T(8,128)} %copy.61), kind=kCustom, calls=%fused_computation.13 | custom fusion | flops 24576 | bytes 311296 | tf_op jit(solution)/shard_map/scatter-add | solution.py:122
  498.0 31.9 %scatter_fusion.2 = f32[6,32768]{0,1:T(8,128)} fusion(f32[6,32768]{0,1:T(8,128)} %scatter_fusion.1, s32[4096]{0:T(1024)S(1)} %copy-done.20, f32[4096,6]{1,0:T(8,128)} %copy.63), kind=kCustom, calls=%fused_computation.14 | custom fusion | flops 24576 | bytes 311296 | tf_op jit(solution)/shard_map/scatter-add | solution.py:122
  529.9 31.9 %scatter_fusion.3 = f32[6,32768]{0,1:T(8,128)} fusion(f32[6,32768]{0,1:T(8,128)} %scatter_fusion.2, s32[4096]{0:T(1024)S(1)} %copy-done.19, f32[4096,6]{1,0:T(8,128)} %copy.65), kind=kCustom, calls=%fused_computation.15 | custom fusion | flops 24576 | bytes 311296 | tf_op jit(solution)/shard_map/scatter-add | solution.py:122
  561.8 31.9 %scatter_fusion.4 = f32[6,32768]{0,1:T(8,128)} fusion(f32[6,32768]{0,1:T(8,128)} %scatter_fusion.3, s32[4096]{0:T(1024)S(1)} %copy-done.18, f32[4096,6]{1,0:T(8,128)} %copy.67), kind=kCustom, calls=%fused_computation.16 | custom fusion | flops 24576 | bytes 311296 | tf_op jit(solution)/shard_map/scatter-add | solution.py:122
  593.7 31.9 %scatter_fusion.5 = f32[6,32768]{0,1:T(8,128)} fusion(f32[6,32768]{0,1:T(8,128)} %scatter_fusion.4, s32[4096]{0:T(1024)S(1)} %copy-done.17, f32[4096,6]{1,0:T(8,128)} %copy.69), kind=kCustom, calls=%fused_computation.17 | custom fusion | flops 24576 | bytes 311296 | tf_op jit(solution)/shard_map/scatter-add | solution.py:122
  625.6 32.1 %scatter_fusion.6 = f32[6,32768]{0,1:T(8,128)} fusion(f32[6,32768]{0,1:T(8,128)} %scatter_fusion.5, s32[4096]{0:T(1024)S(1)} %copy-done.16, f32[4096,6]{1,0:T(8,128)} %copy.71), kind=kCustom, calls=%fused_computation.18 | custom fusion | flops 24576 | bytes 311296 | tf_op jit(solution)/shard_map/scatter-add | solution.py:122
  657.7 31.9 %scatter_fusion.7 = f32[6,32768]{0,1:T(8,128)} fusion(f32[6,32768]{0,1:T(8,128)} %scatter_fusion.6, s32[4096]{0:T(1024)S(1)} %copy-done.15, f32[4096,6]{1,0:T(8,128)} %copy.73), kind=kCustom, calls=%fused_computation.19 | custom fusion | flops 24576 | bytes 311296 | tf_op jit(solution)/shard_map/scatter-add | solution.py:122
  689.6 31.6 %scatter_fusion.8 = f32[6,32768]{0,1:T(8,128)} fusion(f32[6,32768]{0,1:T(8,128)} %scatter_fusion.7, s32[4096]{0:T(1024)S(1)} %copy-done.14, f32[4096,6]{1,0:T(8,128)S(1)} %copy.75), kind=kCustom, calls=%fused_computation.20 | custom fusion | flops 24576 | bytes 311296 | tf_op jit(solution)/shard_map/scatter-add | solution.py:122
  721.2 10.8 %copy.76 = f32[6,1,4,64,128]{4,3,2,1,0:T(8,128)} copy(f32[6,1,4,64,128]{0,4,3,2,1:T(8,128)} %bitcast.157) | data formatting | bytes 1572864 | tf_op jit(solution)/shard_map/reshape | solution.py:123
  (162 shorter events, 23.4 us)
Async XLA Ops:
  0.0 11.1 %copy-start.11 = (s32[4096,1]{0,1:T(1,128)S(1)}, s32[4096,1]{0,1:T(1,128)}, u32[]{:S(2)}) copy-start(s32[4096,1]{0,1:T(1,128)} %param.12) | copy-start | bytes 49156
  0.0 11.3 %copy-start.26 = (s32[4096]{0:T(1024)S(1)}, s32[4096]{0:T(1024)}, u32[]{:S(2)}) copy-start(s32[4096]{0:T(1024)} %param.13) | copy-start | bytes 49156
  0.0 36.1 %copy-start.12 = (f32[3,4096]{1,0:T(4,128)S(1)}, f32[3,4096]{1,0:T(4,128)}, u32[]{:S(2)}) copy-start(f32[3,4096]{1,0:T(4,128)} %param.15) | copy-start | bytes 147460
  0.0 37.5 %copy-start.25 = (s32[4096]{0:T(1024)S(1)}, s32[4096]{0:T(1024)}, u32[]{:S(2)}) copy-start(s32[4096]{0:T(1024)} %param.14) | copy-start | bytes 49156
  0.0 38.2 %copy-start = (f32[6,1,4,64,128]{4,3,2,1,0:T(8,128)S(1)}, f32[6,1,4,64,128]{4,3,2,1,0:T(8,128)}, u32[]{:S(2)}) copy-start(f32[6,1,4,64,128]{4,3,2,1,0:T(8,128)} %param.8) | copy-start | bytes 2359300
  11.4 35.6 %copy-start.22 = (s32[4096,1]{0,1:T(1,128)}, s32[4096,1]{0,1:T(1,128)S(1)}, u32[]{:S(2)}) copy-start(s32[4096,1]{0,1:T(1,128)S(1)} %compare_select_fusion.1) | copy-start | bytes 49156
  27.5 180.2 %all-to-all-start = ((f32[1,32,256]{2,0,1:T(1,128)}), f32[1,32,256]{2,0,1:T(1,128)}, u32[]{:S(2)}, u32[]{:S(2)}) async-start(f32[1,32,256]{2,0,1:T(1,128)} %bitcast.5), calls=%async_computation | async-start | bytes 65536 | tf_op jit(solution)/shard_map/all_to_all | solution.py:109
  167.1 17.8 %copy-start.24 = (f32[1,3,2,6,6]{4,2,3,1,0:T(2,128)S(1)}, f32[1,3,2,6,6]{4,2,3,1,0:T(2,128)}, u32[]{:S(2)}) copy-start(f32[1,3,2,6,6]{4,2,3,1,0:T(2,128)} %param.11) | copy-start | bytes 2596
  207.7 16.9 %all-to-all-start.1 = ((f32[6,32,256]{2,0,1:T(8,128)}), f32[6,32,256]{2,0,1:T(8,128)S(1)}, u32[]{:S(2)}, u32[]{:S(2)}) async-start(f32[6,32,256]{2,0,1:T(8,128)} %copy.51), calls=%async_computation.1 | async-start | bytes 524288 | tf_op jit(solution)/shard_map/all_to_all | solution.py:108
  361.9 6.8 copy-start.2
  361.9 6.8 copy-start.3
  361.9 6.8 copy-start.51
  361.9 6.8 copy-start.52
  361.9 6.8 copy-start.53
  361.9 6.8 copy-start.54
  362.0 6.8 copy-start.55
  362.0 6.8 copy-start.56
  362.0 7.1 copy-start.45
  362.0 7.1 copy-start.46
  362.0 7.1 copy-start.47
  362.0 7.1 copy-start.48
  362.0 7.1 copy-start.49
  362.0 7.1 copy-start.50
  362.1 7.9 %collective-permute-start = (f32[6,1,1,64,128]{4,3,2,1,0:T(8,128)S(1)}, f32[6,1,1,64,128]{4,3,2,1,0:T(8,128)S(1)}, u32[]{:S(2)}, u32[]{:S(2)}) collective-permute-start(f32[6,1,1,64,128]{4,3,2,1,0:T(8,128)S(1)} %get-tuple-element.17), channel_id=1, source_target_pairs={{0,1},{1,2},{2,3},{3,4},{4,5},{5,6},{6,7},{8,9},{9,10},{10,11},{11... | collective-permute-start | bytes 589832 | tf_op jit(solution)/shard_map/ppermute | solution.py:14
  365.6 6.4 collective-permute-start.1
  367.1 2.5 copy-start.39
  367.1 2.5 copy-start.40
  367.1 2.5 copy-start.41
  367.1 2.5 copy-start.42
  367.1 2.5 copy-start.43
  374.7 8.8 %copy-start.13 = (s32[8192]{0:T(1024)S(1)}, s32[8192]{0:T(1024)}, u32[]{:S(2)}) copy-start(s32[8192]{0:T(1024)} %broadcast_clamp_fusion) | copy-start | bytes 98308
  416.9 8.9 %copy-start.23 = (s32[4096,1]{0,1:T(1,128)S(1)}, s32[4096,1]{0,1:T(1,128)}, u32[]{:S(2)}) copy-start(s32[4096,1]{0,1:T(1,128)} %copy-done.22) | copy-start | bytes 49156
  420.5 14.4 %all-to-all-start.2 = ((f32[6,32,256]{2,0,1:T(8,128)}), f32[6,32,256]{2,0,1:T(8,128)S(1)}, u32[]{:S(2)}, u32[]{:S(2)}) async-start(f32[6,32,256]{2,0,1:T(8,128)} %copy.58), calls=%async_computation.2 | async-start | bytes 524288 | tf_op jit(solution)/shard_map/all_to_all | solution.py:118
  437.5 13.7 %copy-start.4 = (f32[1,4096]{1,0:T(1,128)S(1)}, f32[1,4096]{1,0:T(1,128)}, u32[]{:S(2)}) copy-start(f32[1,4096]{1,0:T(1,128)} %get-tuple-element.68) | copy-start | bytes 49156
  437.5 13.7 %copy-start.5 = (f32[1,4096]{1,0:T(1,128)S(1)}, f32[1,4096]{1,0:T(1,128)}, u32[]{:S(2)}) copy-start(f32[1,4096]{1,0:T(1,128)} %get-tuple-element.69) | copy-start | bytes 49156
  437.5 13.7 %copy-start.6 = (f32[1,4096]{1,0:T(1,128)S(1)}, f32[1,4096]{1,0:T(1,128)}, u32[]{:S(2)}) copy-start(f32[1,4096]{1,0:T(1,128)} %get-tuple-element.70) | copy-start | bytes 49156
  437.5 13.7 %copy-start.7 = (f32[1,4096]{1,0:T(1,128)S(1)}, f32[1,4096]{1,0:T(1,128)}, u32[]{:S(2)}) copy-start(f32[1,4096]{1,0:T(1,128)} %get-tuple-element.71) | copy-start | bytes 49156
  437.5 13.7 %copy-start.8 = (f32[1,4096]{1,0:T(1,128)S(1)}, f32[1,4096]{1,0:T(1,128)}, u32[]{:S(2)}) copy-start(f32[1,4096]{1,0:T(1,128)} %get-tuple-element.72) | copy-start | bytes 49156
  437.5 13.7 %copy-start.9 = (f32[1,4096]{1,0:T(1,128)S(1)}, f32[1,4096]{1,0:T(1,128)}, u32[]{:S(2)}) copy-start(f32[1,4096]{1,0:T(1,128)} %get-tuple-element.73) | copy-start | bytes 49156
  437.5 13.7 %copy-start.10 = (f32[1,4096]{1,0:T(1,128)S(1)}, f32[1,4096]{1,0:T(1,128)}, u32[]{:S(2)}) copy-start(f32[1,4096]{1,0:T(1,128)} %get-tuple-element.74) | copy-start | bytes 49156
  463.2 2.6 copy-start.21
  465.2 32.7 %copy-start.20 = (s32[4096]{0:T(1024)S(1)}, s32[4096]{0:T(1024)}, u32[]{:S(2)}) copy-start(s32[4096]{0:T(1024)} %get-tuple-element.91) | copy-start | bytes 49156
  465.9 64.0 %copy-start.19 = (s32[4096]{0:T(1024)S(1)}, s32[4096]{0:T(1024)}, u32[]{:S(2)}) copy-start(s32[4096]{0:T(1024)} %get-tuple-element.92) | copy-start | bytes 49156
  498.0 63.8 %copy-start.18 = (s32[4096]{0:T(1024)S(1)}, s32[4096]{0:T(1024)}, u32[]{:S(2)}) copy-start(s32[4096]{0:T(1024)} %get-tuple-element.90) | copy-start | bytes 49156
  529.9 63.8 %copy-start.17 = (s32[4096]{0:T(1024)S(1)}, s32[4096]{0:T(1024)}, u32[]{:S(2)}) copy-start(s32[4096]{0:T(1024)} %get-tuple-element.94) | copy-start | bytes 49156
  561.8 63.8 %copy-start.16 = (s32[4096]{0:T(1024)S(1)}, s32[4096]{0:T(1024)}, u32[]{:S(2)}) copy-start(s32[4096]{0:T(1024)} %get-tuple-element.96) | copy-start | bytes 49156
  593.7 64.0 %copy-start.15 = (s32[4096]{0:T(1024)S(1)}, s32[4096]{0:T(1024)}, u32[]{:S(2)}) copy-start(s32[4096]{0:T(1024)} %get-tuple-element.95) | copy-start | bytes 49156
  625.6 64.0 %copy-start.14 = (s32[4096]{0:T(1024)S(1)}, s32[4096]{0:T(1024)}, u32[]{:S(2)}) copy-start(s32[4096]{0:T(1024)} %get-tuple-element.81) | copy-start | bytes 49156
  (14 other events, 16.9 us)
where the time goes:
time: 742 us; the launch traced here: 732 us
  local copies, waits for them, and re-layouts  346 us (47%)
  other arithmetic  339 us (46%)
  starting transfers between devices  27 us (4%)
  waiting for transfers between devices  18.4 us (2%)
    scatter-add x8, other arithmetic, per_device(): result = result.at[:, fringe_base + offset].add(weight * returned)  255 us
    gather x16, local copies, waits for them, and re-layouts, per_device(): interp_value = interp_value + weight * flat_field[:, fringe_base + offset]  138 us
    scatter-add x1, other arithmetic, per_device(): merged = flat_field.at[:, landing].add(incoming).reshape(adjoint.shape)  64.3 us
    slice x1, local copies, waits for them, and re-layouts, transpose_apply(): term = factor * grid_field[var][None]  57.7 us
    gather x1, local copies, waits for them, and re-layouts, per_device(): at_receivers = res_flat[:, landing].reshape(var_count, groups, CAP)  33.5 us
    scatter x1, local copies, waits for them, and re-layouts, per_device(): land_slots = jnp.zeros((1, slot_total), jnp.float32).at[:, slot_index].se...  16.1 us
  transfers between devices with their start and end apart: 5, of which 3 were waited for; matrix products, arithmetic and copies ran while one was open for 24% of the time, Pallas kernels for 0%

commit v1 on v0

v1 whole, which is shorter than its diff:
```python
import functools

import jax
import jax.numpy as jnp
from jax import lax
from jax.experimental import pallas as pl
from jax.experimental.pallas import tpu as pltpu
from jax.sharding import PartitionSpec as P

NV, NI, NJ, NK = 6, 4, 64, 128
NR = NI * NJ
R = 4096
G = 32
CAP = 256
F32, BF16, I32 = jnp.float32, jnp.bfloat16, jnp.int32
VMEM = pl.BlockSpec(memory_space=pltpu.VMEM)
NT = (((1,), (1,)), ((), ()))


def split(x):
    hi = x.astype(BF16)
    return hi, (x - hi.astype(F32)).astype(BF16)


def rows(n, m):
    return lax.broadcasted_iota(I32, (n, m), 0)


def corner_rows(base, frac, n):
    i0, j0 = base >> 13, (base >> 7) & 63
    f0, f1 = frac[0:1], frac[1:2]
    jj = rows(NJ, n)
    wj = jnp.where(jj == j0, 1.0 - f1, jnp.where(jj == j0 + 1, f1, 0.0))
    parts = []
    for i in range(NI):
        wi = jnp.where(i0 == i, 1.0 - f0, jnp.where(i0 == i - 1, f0, 0.0))
        parts.append(wj * wi)
    return jnp.concatenate(parts, axis=0)


def corner_cols(base, frac, n):
    k0, f2 = base & 127, frac[2:3]
    kk = rows(NK, n)
    return jnp.where(kk == k0, 1.0 - f2, jnp.where(kk == k0 + 1, f2, 0.0))


def transposed_field(field, ft_ref, copies):
    for v in range(NV):
        hi, lo = split(field(v).T)
        at = pl.ds(v * NK, NK)
        for c, part in enumerate((hi, lo, hi)[:copies]):
            ft_ref[at, c * NR : (c + 1) * NR] = part


def donor_kernel(adj, dest, cell, base, frac, send, rank, ft, vals, pick, *, n, m):
    transposed_field(lambda v: adj[v], ft, 3)

    tri = (rows(256, 256) < lax.broadcasted_iota(I32, (256, 256), 1)).astype(F32).astype(BF16)
    carry = jnp.zeros((G, 1), F32)
    for c in range(R // 256):
        at = slice(c * 256, (c + 1) * 256)
        hot = (rows(G, 256) == dest[:, at]).astype(F32)
        before = jnp.dot(hot.astype(BF16), tri, preferred_element_type=F32) + carry
        carry = carry + jnp.sum(hot, axis=1, keepdims=True)
        rank[:, at] = jnp.sum(hot * before, axis=0, keepdims=True).astype(I32)

    @pl.loop(0, R // n)
    def _(c):
        at = pl.ds(pl.multiple_of(c * n, n), n)
        b, f = base[:, at], frac[:, at]
        hi, lo = split(corner_rows(b, f, n))
        t = jnp.dot(ft[...], jnp.concatenate([hi, hi, lo], axis=0), preferred_element_type=F32)
        wk = corner_cols(b, f, n)
        out = [jnp.sum(t[v * NK : (v + 1) * NK] * wk, axis=0, keepdims=True) for v in range(NV)]
        out += [cell[:, at].astype(F32), jnp.zeros((1, n), F32)]
        vals[:, at] = jnp.concatenate(out, axis=0)

    @pl.loop(0, R // m)
    def _(c):
        at = pl.ds(pl.multiple_of(c * m, m), m)
        hi, lo = split(vals[:, at])
        both = jnp.concatenate([hi.astype(F32), lo.astype(F32)], axis=0)
        to = dest[:, at]
        for d in range(G):
            pick[d * 16 : (d + 1) * 16] = jnp.where(to == d, both, 0.0).astype(BF16)
        place = (rows(CAP, m) == rank[:, at]).astype(F32).astype(BF16)
        t = lax.dot_general(pick[...], place, NT, preferred_element_type=F32)
        t = t.reshape(G, 16, CAP)
        t = t[:, :8] + t[:, 8:]

        @pl.when(c == 0)
        def _():
            send[...] = t

        @pl.when(c > 0)
        def _():
            send[...] += t


def scatter_kernel(adj, got, psi, acc, *, u):
    acc[...] = jnp.zeros_like(acc)

    @pl.loop(0, G // u)
    def _(c):
        left, right = [], [[] for _ in range(NV)]
        for p in range(u):
            g = got[c * u + p]
            cell = g[6:7].astype(I32)
            oi = (rows(NR, CAP) == cell >> 7).astype(F32).astype(BF16)
            ok = rows(NK, CAP) == (cell & 127)
            hi, lo = split(g)
            hi, lo = hi.astype(F32), lo.astype(F32)
            left += [oi, oi]
            for v in range(NV):
                right[v] += [
                    jnp.where(ok, hi[v : v + 1], 0.0).astype(BF16),
                    jnp.where(ok, lo[v : v + 1], 0.0).astype(BF16),
                ]
        left = jnp.concatenate(left, axis=1)
        right = jnp.concatenate([jnp.concatenate(r, axis=1) for r in right], axis=0)
        acc[...] += lax.dot_general(left, right, NT, preferred_element_type=F32)

    for v in range(NV):
        psi[v] = adj[v] + acc[:, v * NK : (v + 1) * NK]


def stencil_kernel(psi, low, high, source, coef, jac, got, res, back, pad, ft, *, tj):
    for v in range(NV):
        pad[v, 0:NJ] = low[v]
        pad[v, NJ : NJ + NR] = psi[v]
        pad[v, NJ + NR :] = high[v]
    kk = lax.broadcasted_iota(I32, (tj, NK), 1)

    @pl.loop(0, NR // tj)
    def _(c):
        r0 = pl.multiple_of(c * tj, tj)
        jj = (rows(tj, NK) + r0) & (NJ - 1)
        total = [[None] * NV for _ in range(3)]
        mid = [pad[v, pl.ds(r0 + NJ, tj)] for v in range(NV)]

        def add(d, s, v, x):
            for e in range(NV):
                term = jac[((d * 2 + s) * NV + v) * NV + e] * x
                total[d][e] = term if total[d][e] is None else total[d][e] + term

        for v in range(NV):
            add(0, 0, v, pad[v, pl.ds(r0 + 2 * NJ, tj)])
            add(0, 1, v, pad[v, pl.ds(r0, tj)])
            add(1, 0, v, jnp.where(jj == NJ - 1, 0.0, pad[v, pl.ds(r0 + NJ + 1, tj)]))
            add(1, 1, v, jnp.where(jj == 0, 0.0, pad[v, pl.ds(r0 + NJ - 1, tj)]))
            add(2, 0, v, jnp.where(kk == NK - 1, 0.0, pltpu.roll(mid[v], NK - 1, 1)))
            add(2, 1, v, jnp.where(kk == 0, 0.0, pltpu.roll(mid[v], 1, 1)))
        at = pl.ds(r0, tj)
        for e in range(NV):
            image = coef[0, at] * mid[e]
            for d in range(3):
                image += coef[d + 1, at] * total[d][e]
            res[e, at] = source[e, at] - image

    transposed_field(lambda v: res[v], ft, 2)

    @pl.loop(0, G)
    def _(s):
        cell = got[s, 6:7].astype(I32)
        oi = (rows(NR, CAP) == cell >> 7).astype(F32).astype(BF16)
        ok = rows(NK, CAP) == (cell & 127)
        t = jnp.dot(ft[...], jnp.concatenate([oi, oi], axis=0), preferred_element_type=F32)
        out = [
            jnp.sum(jnp.where(ok, t[v * NK : (v + 1) * NK], 0.0), axis=0, keepdims=True)
            for v in range(NV)
        ]
        back[s] = jnp.concatenate(out + [jnp.zeros((2, CAP), F32)], axis=0)


def finish_kernel(res, back, rank, dest, base, frac, out, parts, acc, *, n):
    acc[...] = jnp.zeros_like(acc)
    for d in range(G):
        hi, lo = split(back[d])
        parts[d * 16 : (d + 1) * 16] = jnp.concatenate([hi.astype(F32), lo.astype(F32)], axis=0).astype(BF16)

    @pl.loop(0, R // n)
    def _(c):
        at = pl.ds(pl.multiple_of(c * n, n), n)
        place = (rows(CAP, n) == rank[:, at]).astype(F32).astype(BF16)
        t = jnp.dot(parts[...], place, preferred_element_type=F32)
        to = dest[:, at]
        both = jnp.zeros((16, n), F32)
        for d in range(G):
            both = jnp.where(to == d, t[d * 16 : (d + 1) * 16], both)
        value = both[:8] + both[8:]
        b, f = base[:, at], frac[:, at]
        ah, al = split(corner_rows(b, f, n))
        wk = corner_cols(b, f, n)
        left = jnp.concatenate([ah, ah, al], axis=1)
        right = []
        for v in range(NV):
            hi, lo = split(wk * value[v : v + 1])
            right.append(jnp.concatenate([hi, lo, hi], axis=1))
        right = jnp.concatenate(right, axis=0)
        acc[...] += lax.dot_general(left, right, NT, preferred_element_type=F32)

    for v in range(NV):
        out[v] = res[v] + acc[:, v * NK : (v + 1) * NK]


def params():
    return pltpu.CompilerParams(vmem_limit_bytes=48 << 20)


def donor(adj, dest, cell, base, frac, n=512, m=1024):
    return pl.pallas_call(
        functools.partial(donor_kernel, n=n, m=m),
        out_shape=(jax.ShapeDtypeStruct((G, 8, CAP), F32), jax.ShapeDtypeStruct((1, R), I32)),
        in_specs=[VMEM] * 5,
        out_specs=(VMEM, VMEM),
        scratch_shapes=[
            pltpu.VMEM((NV * NK, 3 * NR), BF16),
            pltpu.VMEM((8, R), F32),
            pltpu.VMEM((G * 16, m), BF16),
        ],
        compiler_params=params(),
        name="donor",
    )(adj, dest, cell, base, frac)


def scatter(adj, got, u=2):
    return pl.pallas_call(
        functools.partial(scatter_kernel, u=u),
        out_shape=jax.ShapeDtypeStruct((NV, NR, NK), F32),
        in_specs=[VMEM] * 2,
        out_specs=VMEM,
        scratch_shapes=[pltpu.VMEM((NR, NV * NK), F32)],
        compiler_params=params(),
        name="scatter",
    )(adj, got)


def stencil(psi, low, high, source, coef, jac, got, tj=16):
    return pl.pallas_call(
        functools.partial(stencil_kernel, tj=tj),
        out_shape=(jax.ShapeDtypeStruct((NV, NR, NK), F32), jax.ShapeDtypeStruct((G, 8, CAP), F32)),
        in_specs=[VMEM] * 5 + [pl.BlockSpec(memory_space=pltpu.SMEM), VMEM],
        out_specs=(VMEM, VMEM),
        scratch_shapes=[
            pltpu.VMEM((NV, NR + 2 * NJ, NK), F32),
            pltpu.VMEM((NV * NK, 2 * NR), BF16),
        ],
        compiler_params=params(),
        name="stencil",
    )(psi, low, high, source, coef, jac, got)


def finish(res, back, rank, dest, base, frac, n=512):
    return pl.pallas_call(
        functools.partial(finish_kernel, n=n),
        out_shape=jax.ShapeDtypeStruct((NV, NR, NK), F32),
        in_specs=[VMEM] * 6,
        out_specs=VMEM,
        scratch_shapes=[
            pltpu.VMEM((G * 16, CAP), BF16),
            pltpu.VMEM((NR, NV * NK), F32),
        ],
        compiler_params=params(),
        name="finish",
    )(res, back, rank, dest, base, frac)


def per_device(adjoint, source, cell_coef, flux_jacobian, fringe_dest, fringe_cell, fringe_base, fringe_frac):
    adj = adjoint.reshape(NV, NR, NK)
    src = source.reshape(NV, NR, NK)
    coef = cell_coef.reshape(4, NR, NK)
    jac = flux_jacobian.reshape(3 * 2 * NV * NV)
    dest = fringe_dest.reshape(1, R)
    cell = fringe_cell.reshape(1, R)
    base = fringe_base.reshape(1, R)

    send, rank = donor(adj, dest, cell, base, fringe_frac)
    got = lax.all_to_all(send, "blk", split_axis=0, concat_axis=0, tiled=True)
    psi = scatter(adj, got)
    count = lax.axis_size("sub")
    up = [(i, i + 1) for i in range(count - 1)]
    low = lax.ppermute(psi[:, NR - NJ :], "sub", up)
    high = lax.ppermute(psi[:, :NJ], "sub", [(t, s) for s, t in up])
    res, back = stencil(psi, low, high, src, coef, jac, got)
    back = lax.all_to_all(back, "blk", split_axis=0, concat_axis=0, tiled=True)
    out = finish(res, back, rank, dest, base, fringe_frac)
    return out.reshape(adjoint.shape)


def solution(mesh):
    return jax.shard_map(
        per_device,
        mesh=mesh,
        in_specs=(
            P(None, "blk", "sub", None, None),
            P(None, "blk", "sub", None, None),
            P(None, "blk", "sub", None, None),
            P("blk", None, None, None, None),
            P(("blk", "sub"), None),
            P(("blk", "sub")),
            P(("blk", "sub")),
            P(None, ("blk", "sub")),
        ),
        out_specs=P(None, "blk", "sub", None, None),
        check_vma=False,
    )
```

time: 742 us -> 93.3 us (0.13); the launches traced: 732 us -> 91.8 us
  local copies, waits for them, and re-layouts: 346 us -> 4.29 us
  other arithmetic: 339 us -> 0 us
  Pallas kernels: 0 us -> 47.3 us
  blocking collectives: 0 us -> 30.7 us
  starting transfers between devices: 27 us -> 5.61 us
  waiting for transfers between devices: 18.4 us -> 3.86 us
    scatter-add x9 -> x0, other arithmetic: 320 us -> none  [the longest x8 255 us: per_device(): result = result.at[:, fringe_base + offset].add(weight * returned)]
    gather x19 -> x0, local copies, waits for them, and re-layouts: 185 us -> none  [the longest x16 138 us: per_device(): interp_value = interp_value + weight * flat_field[:, fringe_base + offset]]
    slice x12 -> x1, local copies, waits for them, and re-layouts: 61.3 us -> 0.03 us  [per_device(): high = lax.ppermute(psi[:, :NJ], 'sub', [(t, s) for s, t in up])]
    pallas_call x0 -> x4, Pallas kernels: none -> 47.3 us  [the longest x1 16.1 us: stencil(): pl.pallas_call(functools.partial(stencil_kernel, tj=tj), out_shape=(jax.S...]
    all_to_all x0 -> x2, blocking collectives: none -> 30.7 us  [the longest x1 17.4 us: per_device(): got = lax.all_to_all(send, 'blk', split_axis=0, concat_axis=0, tiled=True)]
    reshape x5 -> x1, local copies, waits for them, and re-layouts: 30.5 us -> 0.11 us  [per_device(): jac = flux_jacobian.reshape(3 * 2 * NV * NV)]
    scatter x2 -> x0, local copies, waits for them, and re-layouts: 29 us -> none  [the longest x1 16.1 us: per_device(): land_slots = jnp.zeros((1, slot_total), jnp.float32).at[:, slot_index].se...]
    all_to_all x3 -> x0, starting transfers between devices: 22 us -> none  [the longest x1 8.64 us: per_device(): lax.all_to_all(land_slots, 'blk', split_axis=1, concat_axis=1, tiled=True)]
  transfers between devices with their start and end apart: 5 -> 2, of which waited for: 3 -> 2; matrix products, arithmetic and copies ran while one was open for 24% -> 0% of each run, Pallas kernels for 0% -> 0%
where the time goes in v1:
time: 93.3 us; the launch traced here: 91.8 us
  Pallas kernels  47.3 us (51%)
  blocking collectives  30.7 us (33%)
  starting transfers between devices  5.61 us (6%)
  local copies, waits for them, and re-layouts  4.29 us (5%)
  waiting for transfers between devices  3.86 us (4%)
    all_to_all x1, blocking collectives, per_device(): got = lax.all_to_all(send, 'blk', split_axis=0, concat_axis=0, tiled=True)  17.4 us
    pallas_call x1, Pallas kernels, stencil(): pl.pallas_call(functools.partial(stencil_kernel, tj=tj), out_shape=(jax.S...  16.1 us
    all_to_all x1, blocking collectives, per_device(): back = lax.all_to_all(back, 'blk', split_axis=0, concat_axis=0, tiled=True)  13.3 us
    pallas_call x1, Pallas kernels, finish(): pl.pallas_call(functools.partial(finish_kernel, n=n), out_shape=jax.Shape...  11.9 us
    pallas_call x1, Pallas kernels, scatter(): pl.pallas_call(functools.partial(scatter_kernel, u=u), out_shape=jax.Shap...  10.1 us
    pallas_call x1, Pallas kernels, donor(): pl.pallas_call(functools.partial(donor_kernel, n=n, m=m), out_shape=(jax....  9.16 us
    ppermute x1, starting transfers between devices, per_device(): low = lax.ppermute(psi[:, NR - NJ:], 'sub', up)  4.19 us
    unnamed x23, local copies, waits for them, and re-layouts  4.16 us
  transfers between devices with their start and end apart: 2, of which 2 were waited for; matrix products, arithmetic and copies ran while one was open for 0% of the time, Pallas kernels for 0%

profile of v1, /device:TPU:1, one launch (start us, length us, event | category | flops | bytes accessed | tf_op | source)
XLA Modules:
  0.0 91.8 jit_solution(10208118950457442247)
XLA Ops:
  0.0 0.0 copy-start
  0.0 1.1 %copy-done = f32[6,1,4,64,128]{4,3,2,1,0:T(8,128)S(1)} copy-done((f32[6,1,4,64,128]{4,3,2,1,0:T(8,128)S(1)}, f32[6,1,4,64,128]{4,3,2,1,0:T(8,128)}, u32[]{:S(2)}) %copy-start) | copy-done | bytes 786456
  1.1 0.0 copy-start.3
  1.1 0.8 copy-done.3
  2.0 0.0 copy-start.5
  2.0 0.7 copy-done.5
  2.7 0.0 copy-start.7
  2.7 0.7 copy-done.7
  3.4 0.0 copy-start.9
  3.4 0.7 copy-done.9
  4.1 9.2 %donor.1 = (f32[32,8,256]{2,1,0:T(8,128)S(1)}, s32[1,4096]{1,0:T(1,128)S(1)}) custom-call(f32[6,256,128]{2,1,0:T(8,128)S(1)} %bitcast.9, s32[1,4096]{1,0:T(1,128)S(1)} %bitcast.13, s32[1,4096]{1,0:T(1,128)S(1)} %bitcast.17, s32[1,4096]{1,0:T(1,128)S(1)} %bitcast.15, f32[3,4096]{1,0:T(4,128)S(1)} %copy-done.3), custom_call_target="tpu_custom_call" | custom-call | tf_op jit(solution)/shard_map/donor/pallas_call | solution.py:211
  13.3 17.4 %all_to_all.10.got = f32[32,8,256]{2,1,0:T(8,128)S(1)} all-to-all(f32[32,8,256]{2,1,0:T(8,128)S(1)} %get-tuple-element.9), channel_id=1, replica_groups=mesh['blk'=32,'sub'=8] {'blk'}, dimensions={0} | all-to-all | bytes 524288 | tf_op jit(solution)/shard_map/all_to_all | solution.py:278
  30.7 0.0 copy-start.10
  30.7 0.0 copy-start.2
  30.7 10.1 %scatter.1.psi = f32[6,256,128]{2,1,0:T(8,128)S(1)} custom-call(f32[6,256,128]{2,1,0:T(8,128)S(1)} %bitcast.10, f32[32,8,256]{2,1,0:T(8,128)S(1)} %all_to_all.10.got), custom_call_target="tpu_custom_call" | custom-call | tf_op jit(solution)/shard_map/scatter/pallas_call | solution.py:227
  40.8 0.0 copy-start.1
  40.8 1.4 %collective-permute-start.1 = (f32[6,64,128]{2,1,0:T(8,128)S(1)}, f32[6,64,128]{2,1,0:T(8,128)S(1)}, u32[]{:S(2)}, u32[]{:S(2)}) collective-permute-start(f32[6,64,128]{2,1,0:T(8,128)S(1)} %get-tuple-element.13), channel_id=1, source_target_pairs={{1,0},{2,1},{3,2},{4,3},{5,4},{6,5},{7,6},{9,8},{10,9},{11,10},{12... | collective-permute-start | bytes 589832 | tf_op jit(solution)/shard_map/ppermute | solution.py:283
  42.3 4.2 %collective-permute-start = (f32[6,64,128]{2,1,0:T(8,128)S(1)}, f32[6,64,128]{2,1,0:T(8,128)S(1)}, u32[]{:S(2)}, u32[]{:S(2)}) collective-permute-start(f32[6,64,128]{2,1,0:T(8,128)S(1)} %get-tuple-element.14), channel_id=1, source_target_pairs={{0,1},{1,2},{2,3},{3,4},{4,5},{5,6},{6,7},{8,9},{9,10},{10,11},{11... | collective-permute-start | bytes 589832 | tf_op jit(solution)/shard_map/ppermute | solution.py:282
  46.4 0.0 copy-done.10
  46.5 0.1 reshape.30.jac
  46.6 3.0 %collective-permute-done.1.high = f32[6,64,128]{2,1,0:T(8,128)S(1)} collective-permute-done((f32[6,64,128]{2,1,0:T(8,128)S(1)}, f32[6,64,128]{2,1,0:T(8,128)S(1)}, u32[]{:S(2)}, u32[]{:S(2)}) %collective-permute-start.1) | collective-permute-done | bytes 196640 | tf_op jit(solution)/shard_map/ppermute | solution.py:283
  49.6 0.9 collective-permute-done.low
  50.4 0.0 copy-done.2
  50.4 0.0 copy-done.1
  50.4 16.1 %stencil.1 = (f32[6,256,128]{2,1,0:T(8,128)S(1)}, f32[32,8,256]{2,1,0:T(8,128)S(1)}) custom-call(f32[6,256,128]{2,1,0:T(8,128)S(1)} %scatter.1.psi, f32[6,64,128]{2,1,0:T(8,128)S(1)} %collective-permute-done.low, f32[6,64,128]{2,1,0:T(8,128)S(1)} %collective-permute-done.1.high, f32[6,256,128]{2,1,0:T(8,128)S(1)} %bitcast.11, f32[4,256,128]{2,1,0:T(8,128)S(1)} %bitcast.12, ...), custom_call_target="tpu_custom_call" | custom-call | tf_op jit(solution)/shard_map/stencil/pallas_call | solution.py:239
  66.6 0.0 copy-start.4
  66.6 0.0 copy-start.6
  66.6 0.0 copy-start.8
  66.6 13.3 %all_to_all.11.back = f32[32,8,256]{2,1,0:T(8,128)S(1)} all-to-all(f32[32,8,256]{2,1,0:T(8,128)S(1)} %get-tuple-element.11), channel_id=1, replica_groups=mesh['blk'=32,'sub'=8] {'blk'}, dimensions={0} | all-to-all | bytes 524288 | tf_op jit(solution)/shard_map/all_to_all | solution.py:285
  79.9 0.0 copy-done.4
  79.9 0.0 copy-done.6
  79.9 0.0 copy-done.8
  79.9 11.9 %finish.1 = f32[6,256,128]{2,1,0:T(8,128)} custom-call(f32[6,256,128]{2,1,0:T(8,128)S(1)} %get-tuple-element.10.res, f32[32,8,256]{2,1,0:T(8,128)S(1)} %all_to_all.11.back, s32[1,4096]{1,0:T(1,128)S(1)} %get-tuple-element.12.rank, s32[1,4096]{1,0:T(1,128)S(1)} %bitcast.14, s32[1,4096]{1,0:T(1,128)S(1)} %bitcast.16, f32[3,4096]{1,0:T(4,128)S(1)} %copy-done.4), custom_call_target="tpu_custom_call" | custom-call | tf_op jit(solution)/shard_map/finish/pallas_call | solution.py:254
  (2 shorter events, 0.0 us)
Async XLA Ops:
  0.0 1.1 %copy-start = (f32[6,1,4,64,128]{4,3,2,1,0:T(8,128)S(1)}, f32[6,1,4,64,128]{4,3,2,1,0:T(8,128)}, u32[]{:S(2)}) copy-start(f32[6,1,4,64,128]{4,3,2,1,0:T(8,128)} %param.8) | copy-start | bytes 2359300
  1.1 0.8 copy-start.3
  2.0 0.7 copy-start.5
  2.7 0.7 copy-start.7
  3.4 0.7 copy-start.9
  30.7 15.8 %copy-start.10 = (f32[1,3,2,6,6]{4,2,3,1,0:T(2,128)S(1)}, f32[1,3,2,6,6]{4,2,3,1,0:T(2,128)}, u32[]{:S(2)}) copy-start(f32[1,3,2,6,6]{4,2,3,1,0:T(2,128)} %param.11) | copy-start | bytes 2596
  30.7 19.8 %copy-start.2 = (f32[4,1,4,64,128]{4,3,2,1,0:T(8,128)S(1)}, f32[4,1,4,64,128]{4,3,2,1,0:T(8,128)}, u32[]{:S(2)}) copy-start(f32[4,1,4,64,128]{4,3,2,1,0:T(8,128)} %param.10) | copy-start | bytes 1572868
  40.8 9.7 %copy-start.1 = (f32[6,1,4,64,128]{4,3,2,1,0:T(8,128)S(1)}, f32[6,1,4,64,128]{4,3,2,1,0:T(8,128)}, u32[]{:S(2)}) copy-start(f32[6,1,4,64,128]{4,3,2,1,0:T(8,128)} %param.9) | copy-start | bytes 2359300
  40.8 8.8 %collective-permute-start.1 = (f32[6,64,128]{2,1,0:T(8,128)S(1)}, f32[6,64,128]{2,1,0:T(8,128)S(1)}, u32[]{:S(2)}, u32[]{:S(2)}) collective-permute-start(f32[6,64,128]{2,1,0:T(8,128)S(1)} %get-tuple-element.13), channel_id=1, source_target_pairs={{1,0},{2,1},{3,2},{4,3},{5,4},{6,5},{7,6},{9,8},{10,9},{11,10},{12... | collective-permute-start | bytes 589832 | tf_op jit(solution)/shard_map/ppermute | solution.py:283
  42.3 8.2 %collective-permute-start = (f32[6,64,128]{2,1,0:T(8,128)S(1)}, f32[6,64,128]{2,1,0:T(8,128)S(1)}, u32[]{:S(2)}, u32[]{:S(2)}) collective-permute-start(f32[6,64,128]{2,1,0:T(8,128)S(1)} %get-tuple-element.14), channel_id=1, source_target_pairs={{0,1},{1,2},{2,3},{3,4},{4,5},{5,6},{6,7},{8,9},{9,10},{10,11},{11... | collective-permute-start | bytes 589832 | tf_op jit(solution)/shard_map/ppermute | solution.py:282
  66.6 13.3 %copy-start.4 = (f32[3,4096]{1,0:T(4,128)S(1)}, f32[3,4096]{1,0:T(4,128)}, u32[]{:S(2)}) copy-start(f32[3,4096]{1,0:T(4,128)} %frac.3) | copy-start | bytes 147460
  66.6 13.3 %copy-start.6 = (s32[4096,1]{0,1:T(1,128)S(1)}, s32[4096,1]{0,1:T(1,128)}, u32[]{:S(2)}) copy-start(s32[4096,1]{0,1:T(1,128)} %param.12) | copy-start | bytes 49156
  66.6 13.3 %copy-start.8 = (s32[4096]{0:T(1024)S(1)}, s32[4096]{0:T(1024)}, u32[]{:S(2)}) copy-start(s32[4096]{0:T(1024)} %param.14) | copy-start | bytes 49156

commit v2 on v1

v2 whole, which is shorter than its diff:
```python
import functools

import jax
import jax.numpy as jnp
from jax import lax
from jax.experimental import pallas as pl
from jax.experimental.pallas import tpu as pltpu
from jax.sharding import PartitionSpec as P

NV, NI, NJ, NK = 6, 4, 64, 128
NR = NI * NJ
R = 4096
G = 32
CAP = 256
F32, BF16, I32 = jnp.float32, jnp.bfloat16, jnp.int32
VMEM = pl.BlockSpec(memory_space=pltpu.VMEM)
MESH = pl.DeviceIdType.MESH
NT = (((1,), (1,)), ((), ()))


def split(x):
    hi = x.astype(BF16)
    return hi, (x - hi.astype(F32)).astype(BF16)


def rows(n, m):
    return lax.broadcasted_iota(I32, (n, m), 0)


def corner_rows(base, frac, n):
    i0, j0 = base >> 13, (base >> 7) & 63
    f0, f1 = frac[0:1], frac[1:2]
    jj = rows(NJ, n)
    wj = jnp.where(jj == j0, 1.0 - f1, jnp.where(jj == j0 + 1, f1, 0.0))
    parts = []
    for i in range(NI):
        wi = jnp.where(i0 == i, 1.0 - f0, jnp.where(i0 == i - 1, f0, 0.0))
        parts.append(wj * wi)
    return jnp.concatenate(parts, axis=0)


def corner_cols(base, frac, n):
    k0, f2 = base & 127, frac[2:3]
    kk = rows(NK, n)
    return jnp.where(kk == k0, 1.0 - f2, jnp.where(kk == k0 + 1, f2, 0.0))


def transposed_field(field, ft_ref, copies):
    for v in range(NV):
        hi, lo = split(field(v).T)
        at = pl.ds(v * NK, NK)
        for c, part in enumerate((hi, lo, hi)[:copies]):
            ft_ref[at, c * NR : (c + 1) * NR] = part


def one_hot(index, n):
    return (rows(n, index.shape[1]) == index).astype(F32).astype(BF16)


def chunk(c, n):
    return pl.ds(pl.multiple_of(c * n, n), n)


def find_ranks(dest, rank):
    tri = (rows(256, 256) < lax.broadcasted_iota(I32, (256, 256), 1)).astype(F32).astype(BF16)

    def step(c, carry):
        at = chunk(c, 256)
        hot = (rows(G, 256) == dest[:, at]).astype(F32)
        before = jnp.dot(hot.astype(BF16), tri, preferred_element_type=F32) + carry
        rank[:, at] = jnp.sum(hot * before, axis=0, keepdims=True).astype(I32)
        return carry + jnp.sum(hot, axis=1, keepdims=True)

    lax.fori_loop(0, R // 256, step, jnp.zeros((G, 1), F32), unroll=True)


def interpolate(ft, cell, base, frac, vals, n, unroll):
    def step(c, _):
        at = chunk(c, n)
        b, f = base[:, at], frac[:, at]
        hi, lo = split(corner_rows(b, f, n))
        t = jnp.dot(ft[...], jnp.concatenate([hi, hi, lo], axis=0), preferred_element_type=F32)
        wk = corner_cols(b, f, n)
        out = [jnp.sum(t[v * NK : (v + 1) * NK] * wk, axis=0, keepdims=True) for v in range(NV)]
        out += [cell[:, at].astype(F32), jnp.zeros((1, n), F32)]
        vals[:, at] = jnp.concatenate(out, axis=0)
        return 0

    lax.fori_loop(0, R // n, step, 0, unroll=unroll)


def pack(vals, dest, rank, pick, send):
    hi, lo = split(vals[...])
    both = jnp.concatenate([hi.astype(F32), lo.astype(F32)], axis=0)
    to = jnp.broadcast_to(dest[...], (16, R))

    def step(d, _):
        pick[pl.ds(pl.multiple_of(d * 16, 16), 16)] = jnp.where(to == d, both, 0.0).astype(BF16)
        return 0

    lax.fori_loop(0, G, step, 0, unroll=4)
    t = lax.dot_general(pick[...], one_hot(rank[...], CAP), NT, preferred_element_type=F32)
    t = t.reshape(G, 16, CAP)
    send[...] = t[:, :8] + t[:, 8:]


def add_received(got, acc, first, count, u):
    def step(c, _):
        left, right = [], [[] for _ in range(count)]
        for p in range(u):
            g = got[c * u + p]
            cell = g[6:7].astype(I32)
            oi = one_hot(cell >> 7, NR)
            ok = one_hot(cell & 127, NK)
            hi, lo = split(g)
            left += [oi, oi]
            for v in range(count):
                at = slice(first + v, first + v + 1)
                right[v] += [ok * hi[at], ok * lo[at]]
        left = jnp.concatenate(left, axis=1)
        right = jnp.concatenate([jnp.concatenate(r, axis=1) for r in right], axis=0)
        acc[...] += lax.dot_general(left, right, NT, preferred_element_type=F32)
        return 0

    acc[...] = jnp.zeros_like(acc)
    lax.fori_loop(0, G // u, step, 0)


def stencil_rows(pad, source, coef, jac, res, first, count, tj):
    kk = lax.broadcasted_iota(I32, (tj, NK), 1)

    def step(c, _):
        r0 = pl.multiple_of(first + c * tj, tj)
        jj = (rows(tj, NK) + r0) & (NJ - 1)
        total = [[None] * NV for _ in range(3)]
        mid = [pad[v, pl.ds(r0 + NJ, tj)] for v in range(NV)]

        def add(d, s, v, x):
            for e in range(NV):
                term = jac[((d * 2 + s) * NV + v) * NV + e] * x
                total[d][e] = term if total[d][e] is None else total[d][e] + term

        for v in range(NV):
            add(0, 0, v, pad[v, pl.ds(r0 + 2 * NJ, tj)])
            add(0, 1, v, pad[v, pl.ds(r0, tj)])
            add(1, 0, v, jnp.where(jj == NJ - 1, 0.0, pad[v, pl.ds(r0 + NJ + 1, tj)]))
            add(1, 1, v, jnp.where(jj == 0, 0.0, pad[v, pl.ds(r0 + NJ - 1, tj)]))
            add(2, 0, v, jnp.where(kk == NK - 1, 0.0, pltpu.roll(mid[v], NK - 1, 1)))
            add(2, 1, v, jnp.where(kk == 0, 0.0, pltpu.roll(mid[v], 1, 1)))
        at = pl.ds(r0, tj)
        for e in range(NV):
            image = coef[0, at] * mid[e]
            for d in range(3):
                image += coef[d + 1, at] * total[d][e]
            res[e, at] = source[e, at] - image
        return 0

    lax.fori_loop(0, count // tj, step, 0)


def unpack_and_add(ret, rank, dest, base, frac, parts, acc, n, unroll):
    for d in range(G):
        hi, lo = split(ret[d])
        parts[d * 16 : (d + 1) * 16] = jnp.concatenate([hi.astype(F32), lo.astype(F32)], axis=0).astype(BF16)

    def step(c, _):
        at = chunk(c, n)
        t = jnp.dot(parts[...], one_hot(rank[:, at], CAP), preferred_element_type=F32)
        to = jnp.broadcast_to(dest[:, at], (16, n))
        both = jnp.zeros((16, n), F32)
        for d in range(G):
            both = jnp.where(to == d, t[d * 16 : (d + 1) * 16], both)
        value = both[:8] + both[8:]
        b, f = base[:, at], frac[:, at]
        ah, al = split(corner_rows(b, f, n))
        wk = corner_cols(b, f, n)
        left = jnp.concatenate([ah, ah, al], axis=1)
        right = []
        for v in range(NV):
            hi, lo = split(wk * value[v : v + 1])
            right.append(jnp.concatenate([hi, lo, hi], axis=1))
        right = jnp.concatenate(right, axis=0)
        acc[...] += lax.dot_general(left, right, NT, preferred_element_type=F32)
        return 0

    acc[...] = jnp.zeros_like(acc)
    lax.fori_loop(0, R // n, step, 0, unroll=unroll)


VG = 2


def kernel(
    adj_h, src_h, coef_h, dest_h, cell_h, base_h, frac_h, jac, out,
    src, coef, dest, cell, base, frac, rank, ft, vals, pick, send, got, back, ret, pad, acc, sums, res, parts,
    load_sem, send1, recv1, send2, recv2, halo_send, halo_recv,
):
    me, z = lax.axis_index("blk"), lax.axis_index("sub")
    nz = lax.axis_size("sub")
    above, below = lax.rem(z + 1, nz), lax.rem(z + nz - 1, nz)
    inner = pad.at[:, NJ : NJ + NR]
    pairs = [
        (dest_h, dest), (adj_h, inner), (base_h, base), (frac_h, frac), (cell_h, cell),
        (coef_h, coef), (src_h, src),
    ]
    loads = [pltpu.make_async_copy(a, b, load_sem.at[i]) for i, (a, b) in enumerate(pairs)]
    for load in loads:
        load.start()

    def peer(o):
        return lax.rem(me + o, G)

    barrier = pltpu.get_barrier_semaphore()

    def greet(o, _):
        pl.semaphore_signal(barrier, inc=1, device_id={"blk": peer(o)}, device_id_type=MESH)
        return 0

    lax.fori_loop(1, G, greet, 0)
    for at in (above, below):
        pl.semaphore_signal(barrier, inc=1, device_id={"sub": at}, device_id_type=MESH)

    loads[0].wait()
    find_ranks(dest, rank)
    for load in loads[1:5]:
        load.wait()
    transposed_field(lambda v: pad[v, NJ : NJ + NR], ft, 3)
    interpolate(ft, cell, base, frac, vals, 256, 8)
    pack(vals, dest, rank, pick, send)

    def put(src_ref, dst_ref, o, ssem, rsem):
        to = peer(o)
        return pltpu.make_async_remote_copy(
            src_ref.at[to], dst_ref.at[me], ssem.at[o], rsem.at[me], device_id={"blk": to}, device_id_type=MESH
        )

    def arrived(src_ref, dst_ref, o, ssem, rsem):
        at = peer(o)
        pltpu.make_async_remote_copy(
            src_ref.at[at], dst_ref.at[at], ssem.at[o], rsem.at[at], device_id={"blk": at}, device_id_type=MESH
        ).wait_recv()

    pl.semaphore_wait(barrier, G + 1)

    def start1(o, _):
        put(send, got, o, send1, recv1).start()
        return 0

    def wait1(o, _):
        arrived(send, got, o, send1, recv1)
        return 0

    lax.fori_loop(1, G, start1, 0)
    got[me] = send[me]
    lax.fori_loop(1, G, wait1, 0)

    halos = []
    for first in range(0, NV, VG):
        add_received(got, acc, first, VG, 8)
        for v in range(VG):
            pad[first + v, NJ : NJ + NR] += acc[:, v * NK : (v + 1) * NK]
        part = pad.at[first : first + VG]
        for d, (lo, hi, to) in enumerate(((NR, 0, above), (NJ, NR + NJ, below))):
            slot = first // VG * 2 + d
            halos.append(
                pltpu.make_async_remote_copy(
                    part.at[:, lo : lo + NJ], part.at[:, hi : hi + NJ], halo_send.at[slot], halo_recv.at[slot],
                    device_id={"sub": to}, device_id_type=MESH,
                )
            )
            halos[-1].start()
    for load in loads[5:]:
        load.wait()
    stencil_rows(pad, src, coef, jac, res, NJ, 2 * NJ, 16)
    for halo in halos:
        halo.wait()

    @pl.when(z == 0)
    def _():
        pad[:, 0:NJ] = jnp.zeros((NV, NJ, NK), F32)

    @pl.when(z == nz - 1)
    def _():
        pad[:, NJ + NR :] = jnp.zeros((NV, NJ, NK), F32)

    stencil_rows(pad, src, coef, jac, res, 0, NJ, 16)
    stencil_rows(pad, src, coef, jac, res, NR - NJ, NJ, 16)

    transposed_field(lambda v: res[v], ft, 2)

    def look_up(o, _):
        s = peer(o)
        cell = got[s, 6:7].astype(I32)
        oi = one_hot(cell >> 7, NR)
        ok = rows(NK, CAP) == (cell & 127)
        t = jnp.dot(ft[:, : 2 * NR], jnp.concatenate([oi, oi], axis=0), preferred_element_type=F32)
        line = [
            jnp.sum(jnp.where(ok, t[v * NK : (v + 1) * NK], 0.0), axis=0, keepdims=True)
            for v in range(NV)
        ]
        back[s] = jnp.concatenate(line + [jnp.zeros((2, CAP), F32)], axis=0)
        return 0

    def group(c, _):
        lax.fori_loop(c * 8 + 1, c * 8 + 9, look_up, 0, unroll=True)

        def start2(o, _):
            put(back, ret, o, send2, recv2).start()
            return 0

        lax.fori_loop(c * 8 + 1, jnp.minimum(c * 8 + 9, G), start2, 0)
        return 0

    lax.fori_loop(0, G // 8, group, 0)
    ret[me] = back[me]

    def wait2(o, _):
        arrived(back, ret, o, send2, recv2)
        return 0

    lax.fori_loop(1, G, wait2, 0)
    unpack_and_add(ret, rank, dest, base, frac, parts, sums, 1024, 2)
    for v in range(NV):
        out[v] = res[v] + sums[:, v * NK : (v + 1) * NK]

    def sent(o, _):
        put(send, got, o, send1, recv1).wait_send()
        put(back, ret, o, send2, recv2).wait_send()
        return 0

    lax.fori_loop(1, G, sent, 0)


def per_device(adjoint, source, cell_coef, flux_jacobian, fringe_dest, fringe_cell, fringe_base, fringe_frac):
    any_space = pl.BlockSpec(memory_space=pl.ANY)
    buffer = pltpu.VMEM((G, 8, CAP), F32)
    line = pltpu.VMEM((1, R), I32)
    field = pltpu.VMEM((NV, NR, NK), F32)
    dma = pltpu.SemaphoreType.DMA
    out = pl.pallas_call(
        kernel,
        out_shape=jax.ShapeDtypeStruct((NV, NR, NK), F32),
        in_specs=[any_space] * 7 + [pl.BlockSpec(memory_space=pltpu.SMEM)],
        out_specs=VMEM,
        scratch_shapes=[
            field, pltpu.VMEM((4, NR, NK), F32), line, line, line, pltpu.VMEM((3, R), F32), line,
            pltpu.VMEM((NV * NK, 3 * NR), BF16), pltpu.VMEM((8, R), F32), pltpu.VMEM((G * 16, R), BF16),
            buffer, buffer, buffer, buffer,
            pltpu.VMEM((NV, NR + 2 * NJ, NK), F32), pltpu.VMEM((NR, VG * NK), F32), pltpu.VMEM((NR, NV * NK), F32),
            field, pltpu.VMEM((G * 16, CAP), BF16),
            dma((7,)), dma((G,)), dma((G,)), dma((G,)), dma((G,)), dma((NV // VG * 2,)), dma((NV // VG * 2,)),
        ],
        compiler_params=pltpu.CompilerParams(vmem_limit_bytes=56 << 20, collective_id=0, has_side_effects=True),
        name="adjoint",
    )(
        adjoint.reshape(NV, NR, NK), source.reshape(NV, NR, NK), cell_coef.reshape(4, NR, NK),
        fringe_dest.reshape(1, R), fringe_cell.reshape(1, R), fringe_base.reshape(1, R), fringe_frac,
        flux_jacobian.reshape(3 * 2 * NV * NV),
    )
    return out.reshape(adjoint.shape)


def solution(mesh):
    return jax.shard_map(
        per_device,
        mesh=mesh,
        in_specs=(
            P(None, "blk", "sub", None, None),
            P(None, "blk", "sub", None, None),
            P(None, "blk", "sub", None, None),
            P("blk", None, None, None, None),
            P(("blk", "sub"), None),
            P(("blk", "sub")),
            P(("blk", "sub")),
            P(None, ("blk", "sub")),
        ),
        out_specs=P(None, "blk", "sub", None, None),
        check_vma=False,
    )
```

time: 93.3 us -> 70 us (0.75); the launches traced: 91.8 us -> 69.8 us
  blocking collectives: 30.7 us -> 0 us
  Pallas kernels: 47.3 us -> 66.3 us
  starting transfers between devices: 5.61 us -> 0 us
  waiting for transfers between devices: 3.86 us -> 0 us
    all_to_all x2 -> x0, blocking collectives: 30.7 us -> none  [the longest x1 17.4 us: per_device(): got = lax.all_to_all(send, 'blk', split_axis=0, concat_axis=0, tiled=True)]
    pallas_call x4 -> x1, Pallas kernels: 47.3 us -> 66.3 us  [per_device(): pl.pallas_call(kernel, out_shape=jax.ShapeDtypeStruct((NV, NR, NK), F32),...]
    ppermute x2 -> x0, starting transfers between devices: 5.61 us -> none  [the longest x1 4.19 us: per_device(): low = lax.ppermute(psi[:, NR - NJ:], 'sub', up)]
    ppermute x2 -> x0, waiting for transfers between devices: 3.86 us -> none  [the longest x1 3 us: per_device(): high = lax.ppermute(psi[:, :NJ], 'sub', [(t, s) for s, t in up])]
    unnamed x23 -> x2, local copies, waits for them, and re-layouts: 4.16 us -> 2.81 us
  transfers between devices with their start and end apart: 2 -> 0, of which waited for: 2 -> 0; matrix products, arithmetic and copies ran while one was open for 0% -> 0% of each run, Pallas kernels for 0% -> 0%
where the time goes in v2:
time: 70 us; the launch traced here: 69.8 us
  Pallas kernels  66.3 us (95%)
  local copies, waits for them, and re-layouts  3.49 us (5%)
    pallas_call x1, Pallas kernels, per_device(): pl.pallas_call(kernel, out_shape=jax.ShapeDtypeStruct((NV, NR, NK), F32),...  66.3 us
    unnamed x2, local copies, waits for them, and re-layouts  2.81 us

profile of v2, /device:TPU:1, one launch (start us, length us, event | category | flops | bytes accessed | tf_op | source)
XLA Modules:
  0.0 69.8 jit_solution(10284500038501993571)
XLA Ops:
  0.0 0.7 %copy.10 = f32[1,3,2,6,6]{4,3,2,1,0:T(8,128)S(1)} copy(f32[1,3,2,6,6]{4,2,3,1,0:T(2,128)} %param.11) | data formatting | bytes 1728 | tf_op args[3]
  0.7 0.7 reshape.30.jac
  1.4 66.3 %adjoint.1 = f32[6,256,128]{2,1,0:T(8,128)} custom-call(f32[6,256,128]{2,1,0:T(8,128)} %bitcast.10, f32[6,256,128]{2,1,0:T(8,128)} %bitcast.11, f32[4,256,128]{2,1,0:T(8,128)} %bitcast.12, s32[1,4096]{1,0:T(1,128)} %bitcast.13, s32[1,4096]{1,0:T(1,128)} %bitcast.14, s32[1,4096]{1,0:T(1,128)} %bitcast.15, f32[3,4096]{1,0:T(4,128)} %frac_h.1, f32[216]{0:T(256)} %reshape.30.jac), custom_call_target="tpu_custom_call" | custom-call | tf_op jit(solution)/shard_map/adjoint/pallas_call | solution.py:340
  67.8 2.1 %copy.13 = f32[6,1,4,64,128]{4,3,2,1,0:T(8,128)} copy(f32[6,1,4,64,128]{4,3,2,1,0:T(8,128)} %bitcast.9) | data formatting | bytes 1572864

commit v3 on v2

v3 whole, which is shorter than its diff:
```python
import functools

import jax
import jax.numpy as jnp
from jax import lax
from jax.experimental import pallas as pl
from jax.experimental.pallas import tpu as pltpu
from jax.sharding import PartitionSpec as P

NV, NI, NJ, NK = 6, 4, 64, 128
NR = NI * NJ
R = 4096
G = 32
CAP = 256
F32, BF16, I32 = jnp.float32, jnp.bfloat16, jnp.int32
VMEM = pl.BlockSpec(memory_space=pltpu.VMEM)
MESH = pl.DeviceIdType.MESH
NT = (((1,), (1,)), ((), ()))


def split(x):
    hi = x.astype(BF16)
    return hi, (x - hi.astype(F32)).astype(BF16)


def rows(n, m):
    return lax.broadcasted_iota(I32, (n, m), 0)


def corner_rows(base, frac, n):
    i0, j0 = base >> 13, (base >> 7) & 63
    f0, f1 = frac[0:1], frac[1:2]
    jj = rows(NJ, n)
    wj = jnp.where(jj == j0, 1.0 - f1, jnp.where(jj == j0 + 1, f1, 0.0))
    parts = []
    for i in range(NI):
        wi = jnp.where(i0 == i, 1.0 - f0, jnp.where(i0 == i - 1, f0, 0.0))
        parts.append(wj * wi)
    return jnp.concatenate(parts, axis=0)


def corner_cols(base, frac, n):
    k0, f2 = base & 127, frac[2:3]
    kk = rows(NK, n)
    return jnp.where(kk == k0, 1.0 - f2, jnp.where(kk == k0 + 1, f2, 0.0))


def transposed_field(field, ft_ref, copies):
    for v in range(NV):
        hi, lo = split(field(v).T)
        at = pl.ds(v * NK, NK)
        for c, part in enumerate((hi, lo, hi)[:copies]):
            ft_ref[at, c * NR : (c + 1) * NR] = part


def one_hot(index, n):
    return (rows(n, index.shape[1]) == index).astype(F32).astype(BF16)


def chunk(c, n):
    return pl.ds(pl.multiple_of(c * n, n), n)


def find_places(dest, place):
    tri = (rows(256, 256) < lax.broadcasted_iota(I32, (256, 256), 1)).astype(F32).astype(BF16)

    def step(c, carry):
        at = chunk(c, 256)
        hot = (rows(G, 256) == dest[:, at]).astype(F32)
        before = jnp.dot(hot.astype(BF16), tri, preferred_element_type=F32) + carry
        place[:, at] = one_hot(jnp.sum(hot * before, axis=0, keepdims=True).astype(I32), CAP)
        return carry + jnp.sum(hot, axis=1, keepdims=True)

    lax.fori_loop(0, R // 256, step, jnp.zeros((G, 1), F32), unroll=True)


def interpolate(ft, cell, base, frac, vals, high, low, cols, n, unroll):
    def step(c, _):
        at = chunk(c, n)
        b, f = base[:, at], frac[:, at]
        hi, lo = split(corner_rows(b, f, n))
        high[:, at], low[:, at] = hi, lo
        t = jnp.dot(ft[...], jnp.concatenate([hi, hi, lo], axis=0), preferred_element_type=F32)
        wk = corner_cols(b, f, n)
        cols[:, at] = wk
        out = [jnp.sum(t[v * NK : (v + 1) * NK] * wk, axis=0, keepdims=True) for v in range(NV)]
        out += [cell[:, at].astype(F32), jnp.zeros((1, n), F32)]
        vals[:, at] = jnp.concatenate(out, axis=0)
        return 0

    lax.fori_loop(0, R // n, step, 0, unroll=unroll)


def pack(vals, dest, place, pick, send):
    hi, lo = split(vals[...])
    both = jnp.concatenate([hi.astype(F32), lo.astype(F32)], axis=0)
    to = jnp.broadcast_to(dest[...], (16, R))

    def step(d, _):
        pick[pl.ds(pl.multiple_of(d * 16, 16), 16)] = jnp.where(to == d, both, 0.0).astype(BF16)
        return 0

    lax.fori_loop(0, G, step, 0, unroll=4)
    t = lax.dot_general(pick[...], place[...], NT, preferred_element_type=F32)
    t = t.reshape(G, 16, CAP)
    send[...] = t[:, :8] + t[:, 8:]


def add_received(got, acc, order, arrive, first, count, u):
    def step(c, _):
        left, right = [], [[] for _ in range(count)]
        for p in range(u):
            if arrive is not None:
                arrive(c * u + p)
            g = got[order(c * u + p)]
            cell = g[6:7].astype(I32)
            oi = one_hot(cell >> 7, NR)
            ok = one_hot(cell & 127, NK)
            hi, lo = split(g)
            left += [oi, oi]
            for v in range(count):
                at = slice(first + v, first + v + 1)
                right[v] += [ok * hi[at], ok * lo[at]]
        left = jnp.concatenate(left, axis=1)
        right = jnp.concatenate([jnp.concatenate(r, axis=1) for r in right], axis=0)
        acc[...] += lax.dot_general(left, right, NT, preferred_element_type=F32)
        return 0

    acc[...] = jnp.zeros_like(acc)
    lax.fori_loop(0, G // u, step, 0)


def stencil_rows(pad, source, coef, jac, res, first, count, tj):
    kk = lax.broadcasted_iota(I32, (tj, NK), 1)

    def step(c, _):
        r0 = pl.multiple_of(first + c * tj, tj)
        jj = (rows(tj, NK) + r0) & (NJ - 1)
        total = [[None] * NV for _ in range(3)]
        mid = [pad[v, pl.ds(r0 + NJ, tj)] for v in range(NV)]

        def add(d, s, v, x):
            for e in range(NV):
                term = jac[d, v, s, e] * x
                total[d][e] = term if total[d][e] is None else total[d][e] + term

        for v in range(NV):
            add(0, 0, v, pad[v, pl.ds(r0 + 2 * NJ, tj)])
            add(0, 1, v, pad[v, pl.ds(r0, tj)])
            add(1, 0, v, jnp.where(jj == NJ - 1, 0.0, pad[v, pl.ds(r0 + NJ + 1, tj)]))
            add(1, 1, v, jnp.where(jj == 0, 0.0, pad[v, pl.ds(r0 + NJ - 1, tj)]))
            add(2, 0, v, jnp.where(kk == NK - 1, 0.0, pltpu.roll(mid[v], NK - 1, 1)))
            add(2, 1, v, jnp.where(kk == 0, 0.0, pltpu.roll(mid[v], 1, 1)))
        at = pl.ds(r0, tj)
        for e in range(NV):
            image = coef[0, at] * mid[e]
            for d in range(3):
                image += coef[d + 1, at] * total[d][e]
            res[e, at] = source[e, at] - image
        return 0

    lax.fori_loop(0, count // tj, step, 0)


def unpack_and_add(ret, place, dest, high, low, cols, parts, acc, n, unroll):
    for d in range(G):
        hi, lo = split(ret[d])
        parts[d * 16 : (d + 1) * 16] = jnp.concatenate([hi.astype(F32), lo.astype(F32)], axis=0).astype(BF16)

    def step(c, _):
        at = chunk(c, n)
        t = jnp.dot(parts[...], place[:, at], preferred_element_type=F32)
        to = jnp.broadcast_to(dest[:, at], (16, n))
        both = jnp.zeros((16, n), F32)
        for d in range(G):
            both = jnp.where(to == d, t[d * 16 : (d + 1) * 16], both)
        value = both[:8] + both[8:]
        ah, al, wk = high[:, at], low[:, at], cols[:, at]
        left = jnp.concatenate([ah, ah, al], axis=1)
        right = []
        for v in range(NV):
            hi, lo = split(wk * value[v : v + 1])
            right.append(jnp.concatenate([hi, lo, hi], axis=1))
        right = jnp.concatenate(right, axis=0)
        acc[...] += lax.dot_general(left, right, NT, preferred_element_type=F32)
        return 0

    acc[...] = jnp.zeros_like(acc)
    lax.fori_loop(0, R // n, step, 0, unroll=unroll)


VG = 2
UP = 8


def kernel(
    adj_h, src_h, coef_h, dest_h, cell_h, base_h, frac_h, jac_h, out,
    src, coef, dest, cell, base, frac, jac, ft, vals, pick, place, high, low, cols,
    send, got, back, ret, pad, rim, acc, sums, res, parts,
    load_sem, send1, recv1, send2, recv2, rim_send, rim_recv,
):
    me, z = lax.axis_index("blk"), lax.axis_index("sub")
    nz = lax.axis_size("sub")
    above, below = lax.rem(z + 1, nz), lax.rem(z + nz - 1, nz)
    inner = pad.at[:, NJ : NJ + NR]
    pairs = [
        (dest_h, dest), (adj_h, inner), (base_h, base), (frac_h, frac), (cell_h, cell),
        (jac_h, jac), (coef_h, coef), (src_h, src),
    ]
    loads = [pltpu.make_async_copy(a, b, load_sem.at[i]) for i, (a, b) in enumerate(pairs)]
    for load in loads:
        load.start()

    def ahead(o):
        return lax.rem(me + o, G)

    def behind(o):
        return lax.rem(me + G - o, G)

    barrier = pltpu.get_barrier_semaphore()

    def greet(o, _):
        pl.semaphore_signal(barrier, inc=1, device_id={"blk": ahead(o)}, device_id_type=MESH)
        return 0

    lax.fori_loop(1, G, greet, 0)
    for at in (above, below):
        pl.semaphore_signal(barrier, inc=1, device_id={"sub": at}, device_id_type=MESH)

    pad[:, 0:NJ] = jnp.zeros((NV, NJ, NK), F32)
    pad[:, NJ + NR :] = jnp.zeros((NV, NJ, NK), F32)
    loads[0].wait()
    find_places(dest, place)
    for load in loads[1:5]:
        load.wait()
    transposed_field(lambda v: pad[v, NJ : NJ + NR], ft, 3)
    interpolate(ft, cell, base, frac, vals, high, low, cols, 256, 8)
    pack(vals, dest, place, pick, send)

    def put(src_ref, dst_ref, n, o, ssem, rsem):
        to = ahead(o)
        return pltpu.make_async_remote_copy(
            src_ref.at[to, 0:n], dst_ref.at[me, 0:n], ssem.at[o], rsem.at[me],
            device_id={"blk": to}, device_id_type=MESH,
        )

    def arrived(src_ref, dst_ref, n, o, ssem, rsem):
        at = behind(o)
        pltpu.make_async_remote_copy(
            src_ref.at[at, 0:n], dst_ref.at[at, 0:n], ssem.at[o], rsem.at[at],
            device_id={"blk": at}, device_id_type=MESH,
        ).wait_recv()

    pl.semaphore_wait(barrier, G + 1)

    def start1(o, _):
        put(send, got, NV + 1, o, send1, recv1).start()
        return 0

    lax.fori_loop(1, G, start1, 0)
    got[me] = send[me]

    def arrive1(o):
        @pl.when(o > 0)
        def _():
            arrived(send, got, NV + 1, o, send1, recv1)

    rims = []
    for first in range(0, NV, VG):
        add_received(got, acc, behind, None if first else arrive1, first, VG, 8)
        for v in range(VG):
            pad[first + v, NJ : NJ + NR] += acc[:, v * NK : (v + 1) * NK]
        part, land = pad.at[first : first + VG], rim.at[:, first : first + VG]
        for d, (row, to) in enumerate(((NR, above), (NJ, below))):
            slot = first // VG * 2 + d
            rims.append(
                pltpu.make_async_remote_copy(
                    part.at[:, row : row + NJ], land.at[d], rim_send.at[slot], rim_recv.at[slot],
                    device_id={"sub": to}, device_id_type=MESH,
                )
            )
            rims[-1].start()
    for load in loads[5:]:
        load.wait()
    stencil_rows(pad, src, coef, jac, res, 0, NR, 16)
    for copy in rims:
        copy.wait()

    def add_rim(d, row):
        def step(c, _):
            at, here = pl.ds(pl.multiple_of(c * 16, 16), 16), pl.ds(pl.multiple_of(row + c * 16, 16), 16)
            for e in range(NV):
                total = jac[0, 0, 1 - d, e] * rim[d, 0, at]
                for v in range(1, NV):
                    total += jac[0, v, 1 - d, e] * rim[d, v, at]
                res[e, here] -= coef[1, here] * total
            return 0

        lax.fori_loop(0, NJ // 16, step, 0)

    @pl.when(z > 0)
    def _():
        add_rim(0, 0)

    @pl.when(z < nz - 1)
    def _():
        add_rim(1, NR - NJ)

    transposed_field(lambda v: res[v], ft, 2)

    def look_up(o):
        s = ahead(o)
        at = got[s, 6:7].astype(I32)
        oi = one_hot(at >> 7, NR)
        ok = rows(NK, CAP) == (at & 127)
        t = jnp.dot(ft[:, : 2 * NR], jnp.concatenate([oi, oi], axis=0), preferred_element_type=F32)
        line = [
            jnp.sum(jnp.where(ok, t[v * NK : (v + 1) * NK], 0.0), axis=0, keepdims=True)
            for v in range(NV)
        ]
        back[s] = jnp.concatenate(line + [jnp.zeros((2, CAP), F32)], axis=0)

    def group(c, _):
        for p in range(UP):
            look_up(c * UP + p + 1)

        def start2(o, _):
            put(back, ret, NV, o, send2, recv2).start()
            return 0

        lax.fori_loop(c * UP + 1, jnp.minimum(c * UP + UP + 1, G), start2, 0)
        return 0

    lax.fori_loop(0, G // UP, group, 0)
    ret[:, NV:] = jnp.zeros((G, 8 - NV, CAP), F32)
    ret[me, 0:NV] = back[me, 0:NV]

    def wait2(o, _):
        arrived(back, ret, NV, o, send2, recv2)
        return 0

    lax.fori_loop(1, G, wait2, 0)
    unpack_and_add(ret, place, dest, high, low, cols, parts, sums, 1024, 2)
    for v in range(NV):
        out[v] = res[v] + sums[:, v * NK : (v + 1) * NK]

    def sent(o, _):
        put(send, got, NV + 1, o, send1, recv1).wait_send()
        put(back, ret, NV, o, send2, recv2).wait_send()
        return 0

    lax.fori_loop(1, G, sent, 0)


def per_device(adjoint, source, cell_coef, flux_jacobian, fringe_dest, fringe_cell, fringe_base, fringe_frac):
    any_space = pl.BlockSpec(memory_space=pl.ANY)
    buffer = pltpu.VMEM((G, 8, CAP), F32)
    line = pltpu.VMEM((1, R), I32)
    field = pltpu.VMEM((NV, NR, NK), F32)
    dma = pltpu.SemaphoreType.DMA
    copies = NV // VG * 2
    arrays = (
        adjoint.reshape(NV, NR, NK), source.reshape(NV, NR, NK), cell_coef.reshape(4, NR, NK),
        fringe_dest.reshape(1, R), fringe_cell.reshape(1, R), fringe_base.reshape(1, R), fringe_frac,
        flux_jacobian[0].transpose(0, 2, 1, 3),
    )
    arrays = [pltpu.with_memory_space_constraint(x, pltpu.HBM) for x in arrays]
    out = pl.pallas_call(
        kernel,
        out_shape=jax.ShapeDtypeStruct((NV, NR, NK), F32),
        in_specs=[any_space] * 8,
        out_specs=VMEM,
        scratch_shapes=[
            field, pltpu.VMEM((4, NR, NK), F32), line, line, line, pltpu.VMEM((3, R), F32),
            pltpu.SMEM((3, NV, 2, NV), F32),
            pltpu.VMEM((NV * NK, 3 * NR), BF16), pltpu.VMEM((8, R), F32), pltpu.VMEM((G * 16, R), BF16),
            pltpu.VMEM((CAP, R), BF16), pltpu.VMEM((NR, R), BF16), pltpu.VMEM((NR, R), BF16), pltpu.VMEM((NK, R), F32),
            buffer, buffer, buffer, buffer,
            pltpu.VMEM((NV, NR + 2 * NJ, NK), F32), pltpu.VMEM((2, NV, NJ, NK), F32),
            pltpu.VMEM((NR, VG * NK), F32), pltpu.VMEM((NR, NV * NK), F32),
            field, pltpu.VMEM((G * 16, CAP), BF16),
            dma((8,)), dma((G,)), dma((G,)), dma((G,)), dma((G,)), dma((copies,)), dma((copies,)),
        ],
        compiler_params=pltpu.CompilerParams(vmem_limit_bytes=48 << 20, collective_id=0, has_side_effects=True),
        name="adjoint",
    )(*arrays)
    return out.reshape(adjoint.shape)


def solution(mesh):
    return jax.shard_map(
        per_device,
        mesh=mesh,
        in_specs=(
            P(None, "blk", "sub", None, None),
            P(None, "blk", "sub", None, None),
            P(None, "blk", "sub", None, None),
            P("blk", None, None, None, None),
            P(("blk", "sub"), None),
            P(("blk", "sub")),
            P(("blk", "sub")),
            P(None, ("blk", "sub")),
        ),
        out_specs=P(None, "blk", "sub", None, None),
        check_vma=False,
    )
```

time: 70 us -> 60.7 us (0.87)
  Pallas kernels: 66.3 us -> 59.7 us
  local copies, waits for them, and re-layouts: 3.49 us -> 0.88 us
    pallas_call x1, Pallas kernels: 66.3 us -> 59.7 us  [per_device(): pl.pallas_call(kernel, out_shape=jax.ShapeDtypeStruct((NV, NR, NK), F32),...]
    unnamed x2 -> x1, local copies, waits for them, and re-layouts: 2.81 us -> 0.88 us
where the time goes in v3:
time: 60.7 us; the launch traced here: 60.6 us
  Pallas kernels  59.7 us (98%)
  local copies, waits for them, and re-layouts  0.88 us (1%)
    pallas_call x1, Pallas kernels, per_device(): pl.pallas_call(kernel, out_shape=jax.ShapeDtypeStruct((NV, NR, NK), F32),...  59.7 us

profile of v3, /device:TPU:1, one launch (start us, length us, event | category | flops | bytes accessed | tf_op | source)
XLA Modules:
  0.0 60.6 jit_solution(1251456256141129208)
XLA Ops:
  0.0 59.7 %adjoint.1 = f32[6,256,128]{2,1,0:T(8,128)S(1)} custom-call(f32[6,256,128]{2,1,0:T(8,128)} %bitcast.13, f32[6,256,128]{2,1,0:T(8,128)} %bitcast.14, f32[4,256,128]{2,1,0:T(8,128)} %bitcast.15, s32[1,4096]{1,0:T(1,128)} %bitcast.17, s32[1,4096]{1,0:T(1,128)} %bitcast.18, s32[1,4096]{1,0:T(1,128)} %bitcast.19, f32[3,4096]{1,0:T(4,128)} %frac_h.1, ...), custom_call_target="tpu_custom_call" | custom-call | tf_op jit(solution)/shard_map/adjoint/pallas_call | solution.py:368
  59.7 0.9 %copy.11 = f32[6,1,4,64,128]{4,3,2,1,0:T(8,128)} copy(f32[6,1,4,64,128]{4,3,2,1,0:T(8,128)S(1)} %bitcast.12) | data formatting | bytes 1572864

commit v4 on v3

--- a/solution.py
+++ b/solution.py
@@ -54,7 +54,9 @@
 
 
 def one_hot(index, n):
-    return (rows(n, index.shape[1]) == index).astype(F32).astype(BF16)
+    m = index.shape[1]
+    hit = rows(n, m).astype(F32).astype(BF16) == index.astype(F32).astype(BF16)
+    return jnp.where(hit, jnp.ones((n, m), BF16), jnp.zeros((n, m), BF16))
 
 
 def chunk(c, n):
@@ -91,28 +93,28 @@
     lax.fori_loop(0, R // n, step, 0, unroll=unroll)
 
 
-def pack(vals, dest, place, pick, send):
-    hi, lo = split(vals[...])
-    both = jnp.concatenate([hi.astype(F32), lo.astype(F32)], axis=0)
-    to = jnp.broadcast_to(dest[...], (16, R))
-
-    def step(d, _):
-        pick[pl.ds(pl.multiple_of(d * 16, 16), 16)] = jnp.where(to == d, both, 0.0).astype(BF16)
-        return 0
-
-    lax.fori_loop(0, G, step, 0, unroll=4)
-    t = lax.dot_general(pick[...], place[...], NT, preferred_element_type=F32)
-    t = t.reshape(G, 16, CAP)
-    send[...] = t[:, :8] + t[:, 8:]
+def pack(vals, offset, place, pick, send, launch):
+    both = jnp.concatenate(split(vals[...]), axis=0)
+    to = jnp.broadcast_to(offset.astype(F32).astype(BF16), (16, R))
+    for o in range(G):
+        pick[o * 16 : (o + 1) * 16] = jnp.where(to == jnp.bfloat16(o), both, jnp.zeros_like(both))
+    part = G // 2
+    for first in (0, part):
+        t = lax.dot_general(pick[first * 16 : (first + part) * 16], place[...], NT, preferred_element_type=F32)
+        t = t.reshape(part, 16, CAP)
+        send[first : first + part] = t[:, :8] + t[:, 8:]
+        for o in range(first, first + part):
+            launch(o)
 
 
 def add_received(got, acc, order, arrive, first, count, u):
     def step(c, _):
         left, right = [], [[] for _ in range(count)]
+        if arrive is not None:
+            for p in range(u):
+                arrive(c * u + p + 1, p == u - 1)
         for p in range(u):
-            if arrive is not None:
-                arrive(c * u + p)
-            g = got[order(c * u + p)]
+            g = got[order(c * u + p + 1)]
             cell = g[6:7].astype(I32)
             oi = one_hot(cell >> 7, NR)
             ok = one_hot(cell & 127, NK)
@@ -223,7 +225,7 @@
         pl.semaphore_signal(barrier, inc=1, device_id={"blk": ahead(o)}, device_id_type=MESH)
         return 0
 
-    lax.fori_loop(1, G, greet, 0)
+    lax.fori_loop(1, G, greet, 0, unroll=True)
     for at in (above, below):
         pl.semaphore_signal(barrier, inc=1, device_id={"sub": at}, device_id_type=MESH)
 
@@ -234,40 +236,44 @@
     for load in loads[1:5]:
         load.wait()
     transposed_field(lambda v: pad[v, NJ : NJ + NR], ft, 3)
-    interpolate(ft, cell, base, frac, vals, high, low, cols, 256, 8)
-    pack(vals, dest, place, pick, send)
-
-    def put(src_ref, dst_ref, n, o, ssem, rsem):
-        to = ahead(o)
+    interpolate(ft, cell, base, frac, vals, high, low, cols, 256, 16)
+    pl.semaphore_wait(barrier, G + 1)
+
+    def put(src, dst_ref, n, o, ssem, rsem):
         return pltpu.make_async_remote_copy(
-            src_ref.at[to, 0:n], dst_ref.at[me, 0:n], ssem.at[o], rsem.at[me],
-            device_id={"blk": to}, device_id_type=MESH,
+            src.at[0:n], dst_ref.at[me, 0:n], ssem.at[o], rsem.at[me],
+            device_id={"blk": ahead(o)}, device_id_type=MESH,
         )
 
-    def arrived(src_ref, dst_ref, n, o, ssem, rsem):
+    def arrived(dst_ref, n, o, ssem, rsem):
         at = behind(o)
         pltpu.make_async_remote_copy(
-            src_ref.at[at, 0:n], dst_ref.at[at, 0:n], ssem.at[o], rsem.at[at],
+            dst_ref.at[at, 0:n], dst_ref.at[at, 0:n], ssem.at[o], rsem.at[at],
             device_id={"blk": at}, device_id_type=MESH,
         ).wait_recv()
 
-    pl.semaphore_wait(barrier, G + 1)
-
-    def start1(o, _):
-        put(send, got, NV + 1, o, send1, recv1).start()
-        return 0
-
-    lax.fori_loop(1, G, start1, 0)
-    got[me] = send[me]
-
-    def arrive1(o):
-        @pl.when(o > 0)
-        def _():
-            arrived(send, got, NV + 1, o, send1, recv1)
+    def put1(o):
+        return put(send.at[o], got, NV + 1, o, send1, recv1)
+
+    def put2(o):
+        return put(back.at[ahead(o)], ret, NV, o, send2, recv2)
+
+    def launch(o):
+        if o:
+            put1(o).start()
+
+    pack(vals, (dest[...] - me) & (G - 1), place, pick, send, launch)
+    got[me] = send[0]
+
+    def arrive1(o, may_be_own):
+        if may_be_own:
+            pl.when(o < G)(lambda: arrived(got, NV + 1, o, send1, recv1))
+        else:
+            arrived(got, NV + 1, o, send1, recv1)
 
     rims = []
     for first in range(0, NV, VG):
-        add_received(got, acc, behind, None if first else arrive1, first, VG, 8)
+        add_received(got, acc, behind, None if first else arrive1, first, VG, 16 if first else 8)
         for v in range(VG):
             pad[first + v, NJ : NJ + NR] += acc[:, v * NK : (v + 1) * NK]
         part, land = pad.at[first : first + VG], rim.at[:, first : first + VG]
@@ -320,36 +326,34 @@
         ]
         back[s] = jnp.concatenate(line + [jnp.zeros((2, CAP), F32)], axis=0)
 
-    def group(c, _):
-        for p in range(UP):
-            look_up(c * UP + p + 1)
-
-        def start2(o, _):
-            put(back, ret, NV, o, send2, recv2).start()
-            return 0
-
-        lax.fori_loop(c * UP + 1, jnp.minimum(c * UP + UP + 1, G), start2, 0)
-        return 0
-
-    lax.fori_loop(0, G // UP, group, 0)
+    ready = []
+    for o in list(range(1, G)):
+        if o % UP == 1:
+            while ready:
+                put2(ready.pop(0)).start()
+        look_up(o)
+        ready.append(o)
+    while ready:
+        put2(ready.pop(0)).start()
+    look_up(0)
+
+    def sent(o, _):
+        put1(o).wait_send()
+        put2(o).wait_send()
+        return 0
+
+    lax.fori_loop(1, G, sent, 0)
     ret[:, NV:] = jnp.zeros((G, 8 - NV, CAP), F32)
     ret[me, 0:NV] = back[me, 0:NV]
 
     def wait2(o, _):
-        arrived(back, ret, NV, o, send2, recv2)
+        arrived(ret, NV, o, send2, recv2)
         return 0
 
     lax.fori_loop(1, G, wait2, 0)
     unpack_and_add(ret, place, dest, high, low, cols, parts, sums, 1024, 2)
     for v in range(NV):
         out[v] = res[v] + sums[:, v * NK : (v + 1) * NK]
-
-    def sent(o, _):
-        put(send, got, NV + 1, o, send1, recv1).wait_send()
-        put(back, ret, NV, o, send2, recv2).wait_send()
-        return 0
-
-    lax.fori_loop(1, G, sent, 0)
 
 
 def per_device(adjoint, source, cell_coef, flux_jacobian, fringe_dest, fringe_cell, fringe_base, fringe_frac):

time: 60.7 us -> 55.2 us (0.909)
  Pallas kernels: 59.7 us -> 54.1 us
    pallas_call x1, Pallas kernels: 59.7 us -> 54.1 us  [per_device(): pl.pallas_call(kernel, out_shape=jax.ShapeDtypeStruct((NV, NR, NK), F32),...]
where the time goes in v4:
time: 55.2 us; the launch traced here: 55 us
  Pallas kernels  54.1 us (98%)
  local copies, waits for them, and re-layouts  0.88 us (2%)
    pallas_call x1, Pallas kernels, per_device(): pl.pallas_call(kernel, out_shape=jax.ShapeDtypeStruct((NV, NR, NK), F32),...  54.1 us

profile of v4, /device:TPU:1, one launch (start us, length us, event | category | flops | bytes accessed | tf_op | source)
XLA Modules:
  0.0 55.0 jit_solution(18176312250620252134)
XLA Ops:
  0.0 54.1 %adjoint.1 = f32[6,256,128]{2,1,0:T(8,128)S(1)} custom-call(f32[6,256,128]{2,1,0:T(8,128)} %bitcast.13, f32[6,256,128]{2,1,0:T(8,128)} %bitcast.14, f32[4,256,128]{2,1,0:T(8,128)} %bitcast.15, s32[1,4096]{1,0:T(1,128)} %bitcast.17, s32[1,4096]{1,0:T(1,128)} %bitcast.18, s32[1,4096]{1,0:T(1,128)} %bitcast.19, f32[3,4096]{1,0:T(4,128)} %frac_h.1, ...), custom_call_target="tpu_custom_call" | custom-call | tf_op jit(solution)/shard_map/adjoint/pallas_call | solution.py:372
  54.1 0.9 %copy.11 = f32[6,1,4,64,128]{4,3,2,1,0:T(8,128)} copy(f32[6,1,4,64,128]{4,3,2,1,0:T(8,128)S(1)} %bitcast.12) | data formatting | bytes 1572864

commit v5 on v4

--- a/solution.py
+++ b/solution.py
@@ -164,7 +164,7 @@
     lax.fori_loop(0, count // tj, step, 0)
 
 
-def unpack_and_add(ret, place, dest, high, low, cols, parts, acc, n, unroll):
+def unpack_and_add(ret, place, dest, high, low, cols, parts, vals, acc, n, unroll):
     for d in range(G):
         hi, lo = split(ret[d])
         parts[d * 16 : (d + 1) * 16] = jnp.concatenate([hi.astype(F32), lo.astype(F32)], axis=0).astype(BF16)
@@ -176,7 +176,14 @@
         both = jnp.zeros((16, n), F32)
         for d in range(G):
             both = jnp.where(to == d, t[d * 16 : (d + 1) * 16], both)
-        value = both[:8] + both[8:]
+        vals[:, at] = both[:8] + both[8:]
+        return 0
+
+    lax.fori_loop(0, R // n, step, 0, unroll=unroll)
+
+    def step(c, _):
+        at = chunk(c, n)
+        value = vals[:, at]
         ah, al, wk = high[:, at], low[:, at], cols[:, at]
         left = jnp.concatenate([ah, ah, al], axis=1)
         right = []
@@ -273,7 +280,7 @@
 
     rims = []
     for first in range(0, NV, VG):
-        add_received(got, acc, behind, None if first else arrive1, first, VG, 16 if first else 8)
+        add_received(got, acc, behind, None if first else arrive1, first, VG, 32 if first else 8)
         for v in range(VG):
             pad[first + v, NJ : NJ + NR] += acc[:, v * NK : (v + 1) * NK]
         part, land = pad.at[first : first + VG], rim.at[:, first : first + VG]
@@ -351,7 +358,7 @@
         return 0
 
     lax.fori_loop(1, G, wait2, 0)
-    unpack_and_add(ret, place, dest, high, low, cols, parts, sums, 1024, 2)
+    unpack_and_add(ret, place, dest, high, low, cols, parts, vals, sums, 1024, 2)
     for v in range(NV):
         out[v] = res[v] + sums[:, v * NK : (v + 1) * NK]
 

time: 55.2 us -> 57.8 us (1.047)
  Pallas kernels: 54.1 us -> 56.7 us
    pallas_call x1, Pallas kernels: 54.1 us -> 56.7 us  [per_device(): pl.pallas_call(kernel, out_shape=jax.ShapeDtypeStruct((NV, NR, NK), F32),...]
where the time goes in v5:
time: 57.8 us; the launch traced here: 57.6 us
  Pallas kernels  56.7 us (98%)
  local copies, waits for them, and re-layouts  0.88 us (2%)
    pallas_call x1, Pallas kernels, per_device(): pl.pallas_call(kernel, out_shape=jax.ShapeDtypeStruct((NV, NR, NK), F32),...  56.7 us

profile of v5, /device:TPU:1, one launch (start us, length us, event | category | flops | bytes accessed | tf_op | source)
XLA Modules:
  0.0 57.6 jit_solution(7036318240151312800)
XLA Ops:
  0.0 56.7 %adjoint.1 = f32[6,256,128]{2,1,0:T(8,128)S(1)} custom-call(f32[6,256,128]{2,1,0:T(8,128)} %bitcast.13, f32[6,256,128]{2,1,0:T(8,128)} %bitcast.14, f32[4,256,128]{2,1,0:T(8,128)} %bitcast.15, s32[1,4096]{1,0:T(1,128)} %bitcast.17, s32[1,4096]{1,0:T(1,128)} %bitcast.18, s32[1,4096]{1,0:T(1,128)} %bitcast.19, f32[3,4096]{1,0:T(4,128)} %frac_h.1, ...), custom_call_target="tpu_custom_call" | custom-call | tf_op jit(solution)/shard_map/adjoint/pallas_call | solution.py:379
  56.7 0.9 %copy.11 = f32[6,1,4,64,128]{4,3,2,1,0:T(8,128)} copy(f32[6,1,4,64,128]{4,3,2,1,0:T(8,128)S(1)} %bitcast.12) | data formatting | bytes 1572864

commit v6 on v5

--- a/solution.py
+++ b/solution.py
@@ -280,7 +280,7 @@
 
     rims = []
     for first in range(0, NV, VG):
-        add_received(got, acc, behind, None if first else arrive1, first, VG, 32 if first else 8)
+        add_received(got, acc, behind, None if first else arrive1, first, VG, 16 if first else 8)
         for v in range(VG):
             pad[first + v, NJ : NJ + NR] += acc[:, v * NK : (v + 1) * NK]
         part, land = pad.at[first : first + VG], rim.at[:, first : first + VG]

time: 57.8 us -> 54.1 us (0.936)
  Pallas kernels: 56.7 us -> 53 us
    pallas_call x1, Pallas kernels: 56.7 us -> 53 us  [per_device(): pl.pallas_call(kernel, out_shape=jax.ShapeDtypeStruct((NV, NR, NK), F32),...]
where the time goes in v6:
time: 54.1 us; the launch traced here: 53.9 us
  Pallas kernels  53 us (98%)
  local copies, waits for them, and re-layouts  0.88 us (2%)
    pallas_call x1, Pallas kernels, per_device(): pl.pallas_call(kernel, out_shape=jax.ShapeDtypeStruct((NV, NR, NK), F32),...  53 us

profile of v6, /device:TPU:1, one launch (start us, length us, event | category | flops | bytes accessed | tf_op | source)
XLA Modules:
  0.0 53.9 jit_solution(1555162150306226688)
XLA Ops:
  0.0 53.0 %adjoint.1 = f32[6,256,128]{2,1,0:T(8,128)S(1)} custom-call(f32[6,256,128]{2,1,0:T(8,128)} %bitcast.13, f32[6,256,128]{2,1,0:T(8,128)} %bitcast.14, f32[4,256,128]{2,1,0:T(8,128)} %bitcast.15, s32[1,4096]{1,0:T(1,128)} %bitcast.17, s32[1,4096]{1,0:T(1,128)} %bitcast.18, s32[1,4096]{1,0:T(1,128)} %bitcast.19, f32[3,4096]{1,0:T(4,128)} %frac_h.1, ...), custom_call_target="tpu_custom_call" | custom-call | tf_op jit(solution)/shard_map/adjoint/pallas_call | solution.py:379
  53.0 0.9 %copy.11 = f32[6,1,4,64,128]{4,3,2,1,0:T(8,128)} copy(f32[6,1,4,64,128]{4,3,2,1,0:T(8,128)S(1)} %bitcast.12) | data formatting | bytes 1572864

commit v7 on v6

--- a/solution.py
+++ b/solution.py
@@ -333,15 +333,15 @@
         ]
         back[s] = jnp.concatenate(line + [jnp.zeros((2, CAP), F32)], axis=0)
 
-    ready = []
-    for o in list(range(1, G)):
-        if o % UP == 1:
-            while ready:
-                put2(ready.pop(0)).start()
-        look_up(o)
-        ready.append(o)
-    while ready:
-        put2(ready.pop(0)).start()
+    def start2(o, _):
+        put2(o).start()
+        return 0
+
+    for first in range(1, G, UP):
+        last = min(first + UP, G)
+        for o in range(first, last):
+            look_up(o)
+        lax.fori_loop(first, last, start2, 0)
     look_up(0)
 
     def sent(o, _):

time: 54.1 us -> 54.3 us (level)
  no operation moved by 1% of the time
where the time goes in v7:
time: 54.3 us; the launch traced here: 54.1 us
  Pallas kernels  53.2 us (98%)
  local copies, waits for them, and re-layouts  0.88 us (2%)
    pallas_call x1, Pallas kernels, per_device(): pl.pallas_call(kernel, out_shape=jax.ShapeDtypeStruct((NV, NR, NK), F32),...  53.2 us

profile of v7, /device:TPU:1, one launch (start us, length us, event | category | flops | bytes accessed | tf_op | source)
XLA Modules:
  0.0 54.1 jit_solution(12371545309714265988)
XLA Ops:
  0.0 53.2 %adjoint.1 = f32[6,256,128]{2,1,0:T(8,128)S(1)} custom-call(f32[6,256,128]{2,1,0:T(8,128)} %bitcast.13, f32[6,256,128]{2,1,0:T(8,128)} %bitcast.14, f32[4,256,128]{2,1,0:T(8,128)} %bitcast.15, s32[1,4096]{1,0:T(1,128)} %bitcast.17, s32[1,4096]{1,0:T(1,128)} %bitcast.18, s32[1,4096]{1,0:T(1,128)} %bitcast.19, f32[3,4096]{1,0:T(4,128)} %frac_h.1, ...), custom_call_target="tpu_custom_call" | custom-call | tf_op jit(solution)/shard_map/adjoint/pallas_call | solution.py:379
  53.2 0.9 %copy.11 = f32[6,1,4,64,128]{4,3,2,1,0:T(8,128)} copy(f32[6,1,4,64,128]{4,3,2,1,0:T(8,128)S(1)} %bitcast.12) | data formatting | bytes 1572864
